TPU v7x, 32 devices: a whole 2x2x4 slice. The times are simulated.
32 devices in a mesh: section: 4 (over y, x), vocab: 8 (over z, core).
Axes of the slice: x: 2, y: 2, z: 4, core: 2. Of those that a mesh axis runs over, the one named last changes fastest.
Arguments:
- exit_hidden: bfloat16 [3, 256, 8192], P(None, 'vocab', 'section')
- norm_gain: float32 [3, 8192], P(None, 'section'), may hold values from 0.5 to 1.5
- head_weight: bfloat16 [8192, 65536], P(None, ('section', 'vocab'))
- teacher: float32 [256, 65536], P('vocab', 'section'), as said below
Outputs:
- divergence: float32 [3], replicated
- grad_hidden: bfloat16 [3, 256, 8192], P(None, 'vocab', 'section')
- grad_head: bfloat16 [8192, 65536], P(None, ('section', 'vocab'))
Inputs may be any that keep to these rules, and one draw needn't show every extreme that they name: Each row of teacher holds log-probabilities: their exponentials sum to one.
All inputs are finite; a program needn't handle non-finite values.
Results may differ from a plain program's by a relative error of at most 0.0086.
Values may be sent and summed in bfloat16 or wider, within the bound.
No kernel may reach another device: no remote copies, remote signals or barrier semaphores. Data moves between devices by JAX's collectives and lax.ppermute only.
A program may use at most 192 MiB of HBM per device.

v0:
```python
import jax
import jax.numpy as jnp
from jax import lax
from jax.sharding import PartitionSpec as P

D = 8192
TOK = 256


epsilon = 1e-05
loss_scale = 1024.0


def body(exit_hidden, norm_gain, head_weight, teacher):
    hidden = exit_hidden.astype(jnp.float32)
    gains = norm_gain[:, None, :]
    squares = lax.psum(jnp.sum(hidden * hidden, axis=-1), "section")
    inverse = lax.rsqrt(squares / D + epsilon)[..., None]
    normed = (hidden * inverse * gains).astype(jnp.bfloat16)
    teacher_cols = lax.all_to_all(teacher, "vocab", split_axis=1, concat_axis=0, tiled=True)
    token_full = lax.all_gather(normed, "vocab", axis=1, tiled=True)
    gathered = lax.all_gather(token_full, "section", axis=2, tiled=True)
    exits_count = gathered.shape[0]
    tokens_count = gathered.shape[1]
    flat_rows = gathered.reshape(exits_count * tokens_count, D)
    local_vocab = head_weight.shape[1]
    logits = jnp.dot(flat_rows, head_weight, preferred_element_type=jnp.float32).reshape(
        exits_count, tokens_count, local_vocab
    )
    target = jnp.exp(teacher_cols)[None]
    cross_local = jnp.sum(target * (teacher_cols[None] - logits), axis=-1)
    weight_local = jnp.sum(target, axis=-1)
    local_max = jnp.max(logits, axis=-1)
    row_max = lax.pmax(local_max, ("section", "vocab"))
    local_total = jnp.sum(jnp.exp(logits - row_max[..., None]), axis=-1)
    exp_total, cross, weight_sum = lax.psum(
        (local_total, cross_local, weight_local), ("section", "vocab")
    )
    log_total = row_max + jnp.log(exp_total)
    divergence = jnp.mean(cross + log_total * weight_sum, axis=-1)
    dlogit = ((jnp.exp(logits - log_total[..., None]) - target) * (loss_scale / TOK)).astype(
        jnp.bfloat16
    )
    flat_dlogit = dlogit.reshape(exits_count * tokens_count, local_vocab)
    grad_head = lax.dot_general(
        flat_rows, flat_dlogit, (((0,), (0,)), ((), ())), preferred_element_type=jnp.float32
    ).astype(jnp.bfloat16)
    partial_value = lax.psum_scatter(
        jnp.einsum("etv,dv->ted", dlogit, head_weight, preferred_element_type=jnp.float32),
        "vocab",
        scatter_dimension=0,
        tiled=True,
    )
    reduced = lax.psum_scatter(partial_value, "section", scatter_dimension=2, tiled=True)
    grad_normed = jnp.transpose(reduced, (1, 0, 2))
    weighted = gains * grad_normed
    inner = lax.psum(jnp.sum(weighted * hidden, axis=-1), "section")[..., None]
    grad_hidden = (inverse * weighted - hidden * inverse**3 * inner / D).astype(jnp.bfloat16)
    return (divergence, grad_hidden, grad_head)


def solution(mesh):
    return jax.shard_map(
        body,
        mesh=mesh,
        in_specs=(
            P(None, "vocab", "section"),
            P(None, "section"),
            P(None, ("section", "vocab")),
            P("vocab", "section"),
        ),
        out_specs=(P(), P(None, "vocab", "section"), P(None, ("section", "vocab"))),
        check_vma=False,
    )
```

profile of v0, /device:TPU:0, one launch (start us, length us, event | category | flops | bytes accessed | tf_op | source)
XLA Modules:
  0.0 650.5 jit_solution(8494987112806706230)
XLA Ops:
  7.2 0.0 all-gather.3.cloned.1.call-start
  7.2 1.1 fusion.8
  8.4 11.4 %psum.35 = f32[3,32]{1,0:T(4,128)S(1)} all-reduce(f32[3,32]{1,0:T(4,128)S(1)} %fusion.8), channel_id=1, replica_groups=mesh['section'=4,'vocab'=8] {'section'}, use_global_device_ids=true, to_apply=%region_1.0 | all-reduce | flops 96 | bytes 768 | tf_op jit(solution)/shard_map/psum | solution.py:17
  19.7 0.6 multiply_multiply_fusion
  20.4 0.0 copy-start.3
  20.4 0.6 copy-done.3
  20.9 1.9 fusion.10
  22.8 0.0 all-gather.3.cloned.1.call-update
  22.9 0.0 all-gather.5.cloned.1.call-start
  22.9 37.7 %all-gather.3.cloned.1.call-done = bf16[3,256,2048]{2,1,0:T(8,128)(2,1)} async-done(((bf16[3,32,2048]{2,1,0:T(8,128)(2,1)}), bf16[3,256,2048]{2,1,0:T(8,128)(2,1)}) %all-gather.3.cloned.1.call-update) | async-done | bytes 3145744 | tf_op jit(solution)/shard_map/all_gather | solution.py:21
  60.6 0.0 all-gather.5.cloned.1.call-update
  60.6 0.0 reduce-scatter.3.cloned.1.call-start
  60.7 1.7 copy.19
  62.4 51.5 %all_to_all.19 = f32[32,8,2048]{2,0,1:T(8,128)S(1)} all-to-all(f32[32,8,2048]{2,0,1:T(8,128)S(1)} %bitcast.32), channel_id=1, replica_groups=mesh['section'=4,'vocab'=8] {'vocab'}, dimensions={1} | all-to-all | bytes 4194304 | tf_op jit(solution)/shard_map/all_to_all | solution.py:20
  113.9 1.7 exp.16
  115.6 0.4 fusion.7
  115.9 0.1 mul.86
  116.0 67.8 %all-gather.5.cloned.1.call-done = bf16[3,256,8192]{2,1,0:T(8,128)(2,1)} async-done(((bf16[3,256,2048]{2,1,0:T(8,128)(2,1)}), bf16[3,256,8192]{2,1,0:T(8,128)(2,1)}) %all-gather.5.cloned.1.call-update) | async-done | bytes 12582928 | tf_op jit(solution)/shard_map/all_gather | solution.py:22
  183.8 35.0 %fusion.16 = (f32[3,256]{1,0:T(4,128)S(1)}, f32[3,256,2048]{2,1,0:T(8,128)}) fusion(bf16[3,256,8192]{2,1,0:T(8,128)(2,1)} %all-gather.5.cloned.1.call-done, bf16[8192,2048]{1,0:T(8,128)(2,1)} %param.6), kind=kOutput, calls=%fused_computation.30 | convolution fusion | flops 25771376640 | bytes 52431872 | tf_op jit(solution)/shard_map/dot_general | solution.py:27
  218.8 39.3 %pmax.7 = f32[3,256]{1,0:T(4,128)S(1)} all-reduce(f32[3,256]{1,0:T(4,128)S(1)} %get-tuple-element.12), channel_id=1, replica_groups=mesh['section'=4,'vocab'=8] {'section','vocab'}, use_global_device_ids=true, to_apply=%region_5.0 | all-reduce | flops 768 | bytes 6144 | tf_op jit(solution)/shard_map/pmax | solution.py:34
  258.1 4.3 exponential_reduce_fusion
  262.3 41.3 %all-reduce = (f32[3,256]{1,0:T(4,128)S(1)}, f32[3,256]{1,0:T(4,128)S(1)}, f32[256]{0:T(256)S(1)}) all-reduce(f32[3,256]{1,0:T(4,128)S(1)} %get-tuple-element.4, f32[3,256]{1,0:T(4,128)S(1)} %get-tuple-element.3, f32[256]{0:T(256)S(1)} %mul.86), channel_id=1, replica_groups=mesh['section'=4,'vocab'=8] {'section','vocab'}, use_global_device_ids=true, to_apply=%region_3.0 | all-reduce | flops 1792 | bytes 14336 | tf_op jit(solution)/shard_map/psum | solution.py:36
  303.6 0.1 add_reduce_fusion
  303.8 35.4 %fusion.4 = f32[256,3,8192]{2,0,1:T(8,128)} fusion(bf16[8192,2048]{1,0:T(8,128)(2,1)} %param.6, f32[3,256,2048]{2,1,0:T(8,128)} %get-tuple-element.13, f32[3,256]{1,0:T(4,128)S(1)} %get-tuple-element.9, f32[256,2048]{1,0:T(8,128)} %exp.16), kind=kOutput, calls=%fused_computation.5 | convolution fusion | flops 25776095232 | bytes 67111936 | tf_op jit(solution)/shard_map/etv,dv->ted/dot_general | solution.py:49
  339.2 0.0 copy-start
  339.2 0.0 reduce-scatter.3.cloned.1.call-update
  339.2 0.3 reduce-scatter.5.cloned.1.call-start
  339.4 246.8 %reduce-scatter.3.cloned.1.call-done = f32[32,3,8192]{2,0,1:T(8,128)} async-done(((f32[256,3,8192]{2,0,1:T(8,128)}), f32[32,3,8192]{2,0,1:T(8,128)}) %reduce-scatter.3.cloned.1.call-update) | async-done | bytes 3145744 | tf_op jit(solution)/shard_map/reduce_scatter | solution.py:48
  586.2 0.0 reduce-scatter.5.cloned.1.call-update
  586.2 0.5 broadcast_multiply_fusion
  586.7 0.0 copy-done
  586.7 0.0 copy-start.1
  586.7 0.0 copy-start.2
  586.8 0.0 copy-start.4
  586.8 0.0 copy-start.5
  586.8 36.7 %bitcast_convert_fusion = bf16[8192,2048]{1,0:T(8,128)(2,1)} fusion(bf16[3,256,8192]{2,1,0:T(8,128)(2,1)} %all-gather.5.cloned.1.call-done, f32[3,256,2048]{2,1,0:T(8,128)} %get-tuple-element.13, f32[3,256]{1,0:T(4,128)S(1)} %get-tuple-element.9, f32[256,2048]{1,0:T(8,128)S(1)} %copy-done), kind=kOutput, calls=%fused_computation | convolution fusion | flops 25792872448 | bytes 54529024 | tf_op jit(solution)/shard_map/dot_general | solution.py:45
  623.4 8.0 %reduce-scatter.5.cloned.1.call-done = f32[32,3,2048]{2,0,1:T(8,128)} async-done(((f32[32,3,8192]{2,0,1:T(8,128)}), f32[32,3,2048]{2,0,1:T(8,128)}) %reduce-scatter.5.cloned.1.call-update) | async-done | bytes 786448 | tf_op jit(solution)/shard_map/reduce_scatter | solution.py:54
  631.5 0.0 copy-done.1
  631.5 0.0 copy-done.2
  631.5 1.4 fusion.15
  632.8 8.9 %psum.39 = f32[3,32]{1,0:T(4,128)S(1)} all-reduce(f32[3,32]{1,0:T(4,128)S(1)} %fusion.15), channel_id=1, replica_groups=mesh['section'=4,'vocab'=8] {'section'}, use_global_device_ids=true, to_apply=%region_14.0 | all-reduce | flops 96 | bytes 768 | tf_op jit(solution)/shard_map/psum | solution.py:57
  641.7 0.0 copy-done.4
  641.7 0.0 copy-done.5
  641.7 2.2 fusion.14
Async XLA Ops:
  7.2 53.4 %all-gather.3.cloned.1.call-start = ((), (), s32[]{:S(2)}) async-start(), calls=%async_computation.3 | async-start | bytes 3538944 | tf_op jit(solution)/shard_map/all_gather | solution.py:21
  20.4 0.6 copy-start.3
  22.9 160.9 %all-gather.5.cloned.1.call-start = ((), (), s32[]{:S(2)}) async-start(), calls=%async_computation.4 | async-start | bytes 15728640 | tf_op jit(solution)/shard_map/all_gather | solution.py:22
  60.6 525.6 %reduce-scatter.3.cloned.1.call-start = ((), (), s32[]{:S(2)}) async-start(), calls=%async_computation.5 | async-start | bytes 28311552 | tf_op jit(solution)/shard_map/reduce_scatter | solution.py:48
  339.2 247.6 %copy-start = (f32[256,2048]{1,0:T(8,128)S(1)}, f32[256,2048]{1,0:T(8,128)}, u32[]{:S(2)}) copy-start(f32[256,2048]{1,0:T(8,128)} %exp.16) | copy-start | bytes 6291460
  339.2 292.3 %reduce-scatter.5.cloned.1.call-start = ((), (), s32[]{:S(2)}) async-start(), calls=%async_computation.6 | async-start | bytes 3932160 | tf_op jit(solution)/shard_map/reduce_scatter | solution.py:54
  586.7 44.7 %copy-start.1 = (bf16[3,32,2048]{2,1,0:T(8,128)(2,1)S(1)}, bf16[3,32,2048]{2,1,0:T(8,128)(2,1)}, u32[]{:S(2)}) copy-start(bf16[3,32,2048]{2,1,0:T(8,128)(2,1)} %param.4) | copy-start | bytes 1179652
  586.7 44.7 %copy-start.2 = (f32[3,2048]{1,0:T(4,128)S(1)}, f32[3,2048]{1,0:T(4,128)}, u32[]{:S(2)}) copy-start(f32[3,2048]{1,0:T(4,128)} %param.5) | copy-start | bytes 73732
  586.8 55.0 %copy-start.4 = (f32[3,32]{1,0:T(4,128)S(1)}, f32[3,32]{1,0:T(4,128)}, u32[]{:S(2)}) copy-start(f32[3,32]{1,0:T(4,128)} %copy-done.3) | copy-start | bytes 1156
  586.8 55.0 %copy-start.5 = (f32[3,32]{1,0:T(4,128)S(1)}, f32[3,32]{1,0:T(4,128)}, u32[]{:S(2)}) copy-start(f32[3,32]{1,0:T(4,128)} %get-tuple-element.10) | copy-start | bytes 1156
Sparse Core Ops, SparseCore 0:
  23.0 37.5 all-gather.2
  62.5 121.2 all-gather.4
  339.3 246.8 reduce-scatter.2
  589.0 42.3 reduce-scatter.4
where the time goes:
time: 651 us
  waiting for transfers between devices  360 us (55%)
  blocking collectives  152 us (23%)
  matrix products  107 us (16%)
  between operations  13.8 us (2%)
  other arithmetic  12.5 us (2%)
    reduce_scatter x1, waiting for transfers between devices, body(): lax.psum_scatter(jnp.einsum('etv,dv->ted', dlogit, head_weight, preferred...  247 us
    all_gather x1, waiting for transfers between devices, body(): gathered = lax.all_gather(token_full, 'section', axis=2, tiled=True)  67.8 us
    all_to_all x1, blocking collectives, body(): lax.all_to_all(teacher, 'vocab', split_axis=1, concat_axis=0, tiled=True)  51.5 us
    psum x1, blocking collectives, body(): lax.psum((local_total, cross_local, weight_local), ('section', 'vocab'))  41.3 us
    pmax x1, blocking collectives, body(): row_max = lax.pmax(local_max, ('section', 'vocab'))  39.3 us
    all_gather x1, waiting for transfers between devices, body(): token_full = lax.all_gather(normed, 'vocab', axis=1, tiled=True)  37.7 us
    dot_general x1, matrix products, body(): lax.dot_general(flat_rows, flat_dlogit, (((0,), (0,)), ((), ())), preferr...  36.7 us
    dot_general x1, matrix products, body(): jnp.einsum('etv,dv->ted', dlogit, head_weight, preferred_element_type=jnp...  35.4 us
  transfers between devices with their start and end apart: 4, of which 4 were waited for; matrix products, arithmetic and copies ran while one was open for 6% of the time, Pallas kernels for 0%

commit v1 on v0

v1 whole, which is shorter than its diff:
```python
import functools
import jax
import jax.numpy as jnp
from jax import lax
from jax.experimental import pallas as pl
from jax.experimental.pallas import tpu as pltpu
from jax.sharding import PartitionSpec as P

epsilon = 1e-05
loss_scale = 1024.0
F32 = jnp.float32
BF16 = jnp.bfloat16
LANES = 128


def swap(x, axis, mask, size):
    return lax.ppermute(x, axis, [(i, i ^ mask) for i in range(size)])


def low(o):
    return o & -o


def high(o):
    return 1 << (o.bit_length() - 1)


def route(o, k):
    return low(o) if k & 1 else high(o)


def gather_order(sections, chips):
    single = [o for o in range(1, sections) if o.bit_count() == 1]
    several = sorted(
        (o for o in range(1, sections) if o.bit_count() > 1), key=lambda o: (o.bit_count(), o)
    )
    seq = []
    for k in range(chips + 1):
        if k < chips:
            seq += [("z", 0, c) for c in range(1, chips) if c ^ low(c) == k]
            seq += [("s", o, k) for o in single]
        if k:
            seq += [("s", o, k - 1) for o in several]
    return seq


def reduce_order(sections, chips):
    return [
        (o, k)
        for count in range(sections.bit_length() - 1, 0, -1)
        for k in reversed(range(chips))
        for o in range(1, sections)
        if o.bit_count() == count
    ]


def merge_kernel(masks, log, *refs):
    own, others, out = refs[0], refs[1:-1], refs[-1]
    n = own.shape[1]
    for b in range(n):
        row = pl.ds(b, 1)
        sources = [(own, row)] + [(r, pl.ds(b ^ m, 1)) for r, m in zip(others, masks)]
        tops = [r[0, at, :] for r, at in sources]
        top = functools.reduce(jnp.maximum, tops)
        total = functools.reduce(
            jnp.add, [r[1, at, :] * jnp.exp(t - top) for (r, at), t in zip(sources, tops)]
        )
        if log:
            out[row, :] = top + jnp.log(total)
        else:
            out[0, row, :] = top
            out[1, row, :] = total


def merge(own, others, masks, log=False):
    return pl.pallas_call(
        functools.partial(merge_kernel, masks, log),
        out_shape=jax.ShapeDtypeStruct(own.shape[1:] if log else own.shape, F32),
        compiler_params=pltpu.CompilerParams(vmem_limit_bytes=4 << 20),
        name="merge",
    )(own, *others)


def logits_kernel(offsets, n_blocks, has_acc, last, *refs):
    n = len(offsets)
    refs = refs[1:]
    pieces, refs = refs[: n * n_blocks], refs[n * n_blocks :]
    weights, refs = refs[:n], refs[n:]
    acc_ref = None
    if has_acc:
        acc_ref, refs = refs[0], refs[1:]
    out_ref, states_ref, stat_ref, refs = refs[0], refs[1], refs[2], refs[3:]
    lhs, in_sem, out_sem = refs[:3]
    rows = pieces[0].shape[0]
    step = pl.program_id(0)
    final = pl.num_programs(0) - 1

    def incoming(g, b):
        return pltpu.make_async_copy(
            pieces[g * n_blocks + b], lhs.at[g, pl.ds(b * rows, rows), :], in_sem.at[g, b]
        )

    def outgoing(g):
        return pltpu.make_async_copy(lhs.at[g], states_ref.at[g], out_sem.at[g])

    @pl.when(step == 0)
    def _():
        for g in range(n):
            for b in range(n_blocks):
                incoming(g, b).start()
        for g in range(n):
            for b in range(n_blocks):
                incoming(g, b).wait()
        for g in range(n):
            outgoing(g).start()

    total = acc_ref[...] if has_acc else None
    for g in range(n):
        part = jnp.dot(lhs[g], weights[g][...], preferred_element_type=F32)
        total = part if total is None else total + part
    out_ref[...] = total
    if last:
        max_ref, sum_ref = refs[3:]
        block_max = jnp.max(total, axis=1, keepdims=True)

        @pl.when(step == 0)
        def _():
            max_ref[...] = jnp.broadcast_to(block_max, max_ref.shape)
            sum_ref[...] = jnp.zeros_like(sum_ref)

        old = max_ref[:, :1]
        new = jnp.maximum(old, block_max)
        fresh = sum_ref[:, :1] * jnp.exp(old - new) + jnp.sum(
            jnp.exp(total - new), axis=1, keepdims=True
        )
        max_ref[...] = jnp.broadcast_to(new, max_ref.shape)
        sum_ref[...] = jnp.broadcast_to(fresh, sum_ref.shape)

    @pl.when(step == final)
    def _():
        for g in range(n):
            outgoing(g).wait()
        if not last:
            stat_ref[...] = jnp.zeros_like(stat_ref)
        else:
            pad = jnp.ones((LANES - rows, LANES), F32)
            for b in range(n_blocks):
                for plane, ref in enumerate((max_ref, sum_ref)):
                    tile = jnp.concatenate([ref[pl.ds(b * rows, rows), :], pad], axis=0)
                    stat_ref[plane, pl.ds(b, 1), :] = tile.T[:1, :]


def logits_part(offsets, position, pieces, weight, acc, last):
    n, n_blocks = len(offsets), len(pieces[0])
    rows, depth = pieces[0][0].shape
    total_rows = n_blocks * rows
    local = weight.shape[1]
    tile = min(512, local)
    any_spec = pl.BlockSpec(memory_space=pl.ANY)
    block = pl.BlockSpec((total_rows, tile), lambda i, pos: (0, i))

    def weight_spec(offset):
        return pl.BlockSpec((depth, tile), lambda i, pos: (pos[offset], i))

    operands = [p for group in pieces for p in group] + [weight] * n
    in_specs = [any_spec] * (n * n_blocks) + [weight_spec(o) for o in offsets]
    if acc is not None:
        operands.append(acc)
        in_specs.append(block)
    out_shape = [
        jax.ShapeDtypeStruct((total_rows, local), F32),
        jax.ShapeDtypeStruct((n, total_rows, depth), BF16),
        jax.ShapeDtypeStruct((2, n_blocks, LANES), F32),
    ]
    out_specs = [block, any_spec, pl.BlockSpec((2, n_blocks, LANES), lambda i, pos: (0, 0, 0))]
    scratch = [
        pltpu.VMEM((n, total_rows, depth), BF16),
        pltpu.SemaphoreType.DMA((n, n_blocks)),
        pltpu.SemaphoreType.DMA((n,)),
    ]
    if last:
        scratch += [pltpu.VMEM((total_rows, LANES), F32)] * 2
    return pl.pallas_call(
        functools.partial(logits_kernel, offsets, n_blocks, acc is not None, last),
        grid_spec=pltpu.PrefetchScalarGridSpec(
            num_scalar_prefetch=1,
            grid=(local // tile,),
            in_specs=in_specs,
            out_specs=out_specs,
            scratch_shapes=scratch,
        ),
        out_shape=out_shape,
        compiler_params=pltpu.CompilerParams(vmem_limit_bytes=32 << 20),
        cost_estimate=pl.CostEstimate(
            flops=2 * n * total_rows * depth * local,
            bytes_accessed=n * depth * local * 2 + total_rows * local * 8,
            transcendentals=0,
        ),
    )(position, *operands)


def delta_kernel(exits, scale, logits_ref, teacher_ref, norm_ref, delta_ref, div_ref):
    b = pl.program_id(0)

    @pl.when(b == 0)
    def _():
        div_ref[...] = jnp.zeros_like(div_ref)

    rows = logits_ref.shape[0]
    tokens = rows // exits
    line = jnp.broadcast_to(norm_ref[pl.ds(b, 1), :], (LANES, LANES))
    column = line.T[:rows, :1]
    teacher = teacher_ref[0]
    target = jnp.exp(teacher)
    for e in range(exits):
        part = pl.ds(e * tokens, tokens)
        shifted = logits_ref[part, :] - column[e * tokens : (e + 1) * tokens]
        delta_ref[part, :] = ((jnp.exp(shifted) - target) * scale).astype(BF16)
        gap = jnp.sum(target * (teacher - shifted), axis=0, keepdims=True)
        gap = jnp.sum(gap, axis=1, keepdims=True)
        div_ref[pl.ds(e, 1), :] += jnp.broadcast_to(gap, (1, LANES))


def delta_pass(logits, teacher, log_total, exits, scale):
    total_rows, local = logits.shape
    n_blocks, tokens, _ = teacher.shape
    rows = exits * tokens
    return pl.pallas_call(
        functools.partial(delta_kernel, exits, scale),
        grid=(n_blocks,),
        in_specs=[
            pl.BlockSpec((rows, local), lambda b: (b, 0)),
            pl.BlockSpec((1, tokens, local), lambda b: (b, 0, 0)),
            pl.BlockSpec((n_blocks, LANES), lambda b: (0, 0)),
        ],
        out_specs=[
            pl.BlockSpec((rows, local), lambda b: (b, 0)),
            pl.BlockSpec((8, LANES), lambda b: (0, 0)),
        ],
        out_shape=[
            jax.ShapeDtypeStruct((total_rows, local), BF16),
            jax.ShapeDtypeStruct((8, LANES), F32),
        ],
        compiler_params=pltpu.CompilerParams(vmem_limit_bytes=16 << 20),
        cost_estimate=pl.CostEstimate(
            flops=total_rows * local * 8,
            bytes_accessed=total_rows * local * 6 + n_blocks * tokens * local * 4,
            transcendentals=total_rows * local,
        ),
        name="delta",
    )(logits, teacher, log_total)


def state_grad_kernel(n_blocks, n_after, *refs):
    delta_ref, weight_ref = refs[1:3]
    keep_ref, send_ref = refs[3 + n_after :]
    rows = delta_ref.shape[0] // n_blocks
    part = lax.dot_general(
        delta_ref[...], weight_ref[...], (((1,), (1,)), ((), ())), preferred_element_type=F32
    ).astype(BF16)
    for b in range(n_blocks):
        target = send_ref if b & 1 else keep_ref
        target[b >> 1] = part[b * rows : (b + 1) * rows]


def state_grad(offset, position, delta, weight, n_blocks, sections, after):
    total_rows, local = delta.shape
    rows = total_rows // n_blocks
    depth = weight.shape[0] // sections
    tile = min(512, depth)
    steps = depth // tile
    spec = pl.BlockSpec((n_blocks // 2, rows, tile), lambda i, pos: (0, 0, i))
    shape = jax.ShapeDtypeStruct((n_blocks // 2, rows, depth), BF16)
    return pl.pallas_call(
        functools.partial(state_grad_kernel, n_blocks, len(after)),
        grid_spec=pltpu.PrefetchScalarGridSpec(
            num_scalar_prefetch=1,
            grid=(steps,),
            in_specs=[
                pl.BlockSpec(
                    (total_rows, local), lambda i, pos: (0, 0), pipeline_mode=pl.Buffered(1)
                ),
                pl.BlockSpec((tile, local), lambda i, pos: (pos[offset] * steps + i, 0)),
            ]
            + [pl.BlockSpec(memory_space=pl.ANY)] * len(after),
            out_specs=[spec, spec],
        ),
        out_shape=[shape, shape],
        compiler_params=pltpu.CompilerParams(vmem_limit_bytes=24 << 20),
        cost_estimate=pl.CostEstimate(
            flops=2 * total_rows * depth * local,
            bytes_accessed=depth * (local + total_rows) * 2 + total_rows * local * 2,
            transcendentals=0,
        ),
    )(position, delta, weight, *after)


def head_grad_kernel(*refs):
    states_ref, delta_ref = refs[1:3]
    refs[-1][...] = lax.dot_general(
        states_ref[0], delta_ref[...], (((0,), (0,)), ((), ())), preferred_element_type=F32
    ).astype(BF16)


def head_grad(offset, position, states, index, delta, out, after, sections):
    _, total_rows, depth = states.shape
    local = delta.shape[1]
    tile = min(512, depth)
    steps = depth // tile
    extra = list(after) + ([] if out is None else [out])
    return pl.pallas_call(
        head_grad_kernel,
        grid_spec=pltpu.PrefetchScalarGridSpec(
            num_scalar_prefetch=1,
            grid=(steps,),
            in_specs=[
                pl.BlockSpec((1, total_rows, tile), lambda i, pos: (index, 0, i)),
                pl.BlockSpec(
                    (total_rows, local), lambda i, pos: (0, 0), pipeline_mode=pl.Buffered(1)
                ),
            ]
            + [pl.BlockSpec(memory_space=pl.ANY)] * len(extra),
            out_specs=pl.BlockSpec((tile, local), lambda i, pos: (pos[offset] * steps + i, 0)),
        ),
        out_shape=jax.ShapeDtypeStruct((sections * depth, local), BF16),
        input_output_aliases={} if out is None else {2 + len(extra): 0},
        compiler_params=pltpu.CompilerParams(vmem_limit_bytes=24 << 20),
        cost_estimate=pl.CostEstimate(
            flops=2 * total_rows * depth * local,
            bytes_accessed=depth * (local + total_rows) * 2 + total_rows * local * 2,
            transcendentals=0,
        ),
    )(position, states, delta, *extra)


def body(sections, vocabs, exit_hidden, norm_gain, head_weight, teacher):
    chips = vocabs // 2
    exits, tokens, depth = exit_hidden.shape
    rows = exits * tokens
    local = head_weight.shape[1]
    width = depth * sections
    all_tokens = tokens * vocabs
    section = lax.axis_index("section")
    vocab = lax.axis_index("vocab")
    position = jnp.stack([section ^ o for o in range(sections)]).astype(jnp.int32)

    def sec(x, mask):
        return swap(x, "section", mask, sections)

    def voc(x, mask):
        return swap(x, "vocab", mask, vocabs)

    def sec_sum(x):
        return functools.reduce(jnp.add, [x] + [sec(x, o) for o in range(1, sections)])

    hidden = exit_hidden.astype(F32)
    gains = norm_gain[:, None, :]
    squares = sec_sum(jnp.sum(hidden * hidden, axis=-1))
    inverse = lax.rsqrt(squares / width + epsilon)[..., None]
    normed = (hidden * inverse * gains).astype(BF16).reshape(rows, depth)

    order = sorted(range(sections), key=lambda o: (o.bit_count(), o))
    mine = [[None] * chips for _ in range(sections)]
    theirs = [[None] * chips for _ in range(sections)]
    mine[0][0] = normed
    sequence = gather_order(sections, chips)
    late = [step for step in sequence if step[0] == "s" and step[1].bit_count() > 1]
    late = [step for step in late if step[2] >= chips // 2]

    def gather(kind, o, k, token=None):
        if kind == "z":
            source, bit = mine[0][k ^ low(k)], low(k)
        else:
            bit = route(o, k)
            source = mine[o ^ bit][k]
        if token is not None:
            source, _ = lax.optimization_barrier((source, token))
        mine[o][k] = voc(source, 2 * bit) if kind == "z" else sec(source, bit)

    for step in sequence:
        if step not in late:
            gather(*step)
    for k in range(chips):
        theirs[0][k] = voc(mine[0][k], 1)

    def column_block(mask):
        return lax.dynamic_slice_in_dim(teacher, (vocab ^ mask) * local, local, axis=1)

    keep = [column_block(2 * k) for k in range(chips)]
    other = voc(jnp.stack([column_block(2 * k + 1) for k in range(chips)]), 1)
    teacher_blocks = [jnp.stack([keep[0], other[0]])]
    for k in range(1, chips):
        pair = jnp.stack([keep[k], other[k]])
        pair, _ = lax.optimization_barrier((pair, mine[0][-1]))
        teacher_blocks.append(voc(pair, 2 * k))
    teacher_cols = jnp.concatenate(teacher_blocks, axis=0)

    groups = []
    for o in order:
        if groups and groups[-1][0].bit_count() == o.bit_count():
            groups[-1].append(o)
        else:
            groups.append([o])
    acc, states = None, {}
    for index, group in enumerate(groups):
        pieces = [
            [(theirs if b & 1 else mine)[o][b >> 1] for b in range(vocabs)] for o in group
        ]
        result = logits_part(
            group, position, pieces, head_weight, acc, index == len(groups) - 1
        )
        acc, block_states, stats = result
        for g, o in enumerate(group):
            states[o] = (block_states, g)
        if index == 0:
            for step in late:
                gather(*step, token=stats)
            for o in order[1:]:
                for k in range(chips):
                    block, _ = lax.optimization_barrier((mine[o][k], stats))
                    theirs[o][k] = voc(block, 1)
    logits = acc

    others = [sec(stats, o) for o in range(1, sections)]
    stats = merge(stats, others, [0] * len(others))
    others = [voc(stats, 2 * k) for k in range(1, chips)]
    stats = merge(stats, others, [2 * k for k in range(1, chips)])
    log_total = merge(stats, [voc(stats, 1)], [1], log=True)

    delta, gaps = delta_pass(logits, teacher_cols, log_total, exits, loss_scale / all_tokens)

    kept, got, moved = {}, {}, {}

    def total_of(o, k):
        total = kept[o][k].astype(F32) + got[o][k].astype(F32)
        for block in moved.get((o, k), ()):
            total = total + block.astype(F32)
        return total

    def send(todo):
        packed = [total_of(o, k).astype(BF16) for o, k in todo]
        for (o, k), block in zip(todo, packed):
            bit = route(o, k)
            moved.setdefault((o ^ bit, k), []).append(sec(block, bit))
        return packed

    backward = list(reversed(order))
    sends = reduce_order(sections, chips)
    first = [step for step in sends if step[0] == backward[0]]
    after = []
    for index, o in enumerate(backward):
        kept[o], sent = state_grad(o, position, delta, head_weight, vocabs, sections, after)
        got[o] = voc(sent, 1)
        after = [kept[o]]
        if index == 1:
            after += send(first)
    rest = [step for step in sends if step not in first]
    for count in range(sections.bit_length() - 1, 0, -1):
        for k in reversed(range(chips)):
            after += send([step for step in rest if step[0].bit_count() == count and step[1] == k])

    sums = {}
    chain = []
    for k in range(chips - 1, 0, -1):
        total = sums.pop(k, 0.0) + total_of(0, k)
        packed = total.astype(BF16)
        chain.append(packed)
        sums[k ^ low(k)] = sums.get(k ^ low(k), 0.0) + voc(packed, 2 * low(k)).astype(F32)
    own_sum = sums[0] + total_of(0, 0)

    share = -(-len(chain) // (sections - 1))
    grad_head = None
    for o in range(sections):
        if o:
            after = chain[(o - 1) * share : o * share]
        block_states, index = states[o]
        grad_head = head_grad(
            o, position, block_states, index, delta, grad_head, after, sections
        )

    gap = gaps[:, :1].reshape(1, 8)
    for index in range(vocabs.bit_length() - 1):
        gap, _ = lax.optimization_barrier((gap, chain[min(index, len(chain) - 1)]))
        gap = gap + voc(gap, 1 << index)

    grad_normed = own_sum.reshape(exits, tokens, depth)
    weighted = gains * grad_normed
    inner = jnp.sum(weighted * hidden, axis=-1)
    gap_row = jnp.pad(gap[:, :exits], ((0, 0), (0, tokens - exits)))
    joined = sec_sum(jnp.concatenate([inner, gap_row], axis=0))
    divergence = joined[exits, :exits] / all_tokens
    inner = joined[:exits][..., None]
    grad_hidden = (inverse * weighted - hidden * inverse**3 * inner / width).astype(BF16)
    return divergence, grad_hidden, grad_head


def solution(mesh):
    sections, vocabs = mesh.shape["section"], mesh.shape["vocab"]
    return jax.shard_map(
        functools.partial(body, sections, vocabs),
        mesh=mesh,
        in_specs=(
            P(None, "vocab", "section"),
            P(None, "section"),
            P(None, ("section", "vocab")),
            P("vocab", "section"),
        ),
        out_specs=(P(), P(None, "vocab", "section"), P(None, ("section", "vocab"))),
        check_vma=False,
    )
```

time: 651 us -> 297 us (0.46)
  waiting for transfers between devices: 360 us -> 83.1 us
  blocking collectives: 152 us -> 0 us
  Pallas kernels: 0 us -> 132 us
  matrix products: 107 us -> 0 us
  starting transfers between devices: 0.38 us -> 58 us
  between operations: 13.8 us -> 1.14 us
  local copies, waits for them, and re-layouts: 4.09 us -> 12.3 us
    reduce_scatter x2 -> x0, waiting for transfers between devices: 255 us -> none  [the longest x1 247 us: body(): lax.psum_scatter(jnp.einsum('etv,dv->ted', dlogit, head_weight, preferred...]
    pallas_call x0 -> x15, Pallas kernels: none -> 132 us  [the longest x3 50.5 us: logits_part(): pl.pallas_call(functools.partial(logits_kernel, offsets, n_blocks, acc is...]
    dot_general x3 -> x0, matrix products: 107 us -> none  [the longest x1 36.7 us: body(): lax.dot_general(flat_rows, flat_dlogit, (((0,), (0,)), ((), ())), preferr...]
    all_gather x2 -> x0, waiting for transfers between devices: 105 us -> none  [the longest x1 67.8 us: body(): gathered = lax.all_gather(token_full, 'section', axis=2, tiled=True)]
    ppermute x0 -> x70, waiting for transfers between devices: none -> 83.1 us  [swap(): return lax.ppermute(x, axis, [(i, i ^ mask) for i in range(size)])]
    psum x3 -> x0, blocking collectives: 61.6 us -> none  [the longest x1 41.3 us: body(): lax.psum((local_total, cross_local, weight_local), ('section', 'vocab'))]
    ppermute x0 -> x70, starting transfers between devices: none -> 58 us  [swap(): return lax.ppermute(x, axis, [(i, i ^ mask) for i in range(size)])]
    all_to_all x1 -> x0, blocking collectives: 51.5 us -> none  [body(): lax.all_to_all(teacher, 'vocab', split_axis=1, concat_axis=0, tiled=True)]
  transfers between devices with their start and end apart: 4 -> 70, of which waited for: 4 -> 22; matrix products, arithmetic and copies ran while one was open for 6% -> 4% of each run, Pallas kernels for 0% -> 40%
where the time goes in v1:
time: 297 us; the launch traced here: 296 us
  Pallas kernels  132 us (44%)
  waiting for transfers between devices  83.1 us (28%)
  starting transfers between devices  58 us (20%)
  local copies, waits for them, and re-layouts  12.3 us (4%)
  other arithmetic  9.36 us (3%)
    ppermute x70, waiting for transfers between devices, swap(): return lax.ppermute(x, axis, [(i, i ^ mask) for i in range(size)])  83.1 us
    ppermute x70, starting transfers between devices, swap(): return lax.ppermute(x, axis, [(i, i ^ mask) for i in range(size)])  58 us
    pallas_call x3, Pallas kernels, logits_part(): pl.pallas_call(functools.partial(logits_kernel, offsets, n_blocks, acc is...  50.5 us
    pallas_call x4, Pallas kernels, state_grad(): pl.pallas_call(functools.partial(state_grad_kernel, n_blocks, len(after))...  39 us
    pallas_call x4, Pallas kernels, head_grad(): pl.pallas_call(head_grad_kernel, grid_spec=pltpu.PrefetchScalarGridSpec(n...  38.3 us
    unnamed x41, local copies, waits for them, and re-layouts  7.53 us
  transfers between devices with their start and end apart: 70, of which 22 were waited for; matrix products, arithmetic and copies ran while one was open for 4% of the time, Pallas kernels for 40%

profile of v1, /device:TPU:0, one launch (start us, length us, event | category | flops | bytes accessed | tf_op | source)
XLA Modules:
  0.0 296.2 jit_solution(17231140241017438812)
XLA Ops:
  0.6 1.1 fusion
  1.8 4.0 %collective-permute-start.2 = (f32[3,32]{1,0:T(4,128)S(1)}, f32[3,32]{1,0:T(4,128)S(1)}, u32[]{:S(2)}, u32[]{:S(2)}) collective-permute-start(f32[3,32]{1,0:T(4,128)S(1)} %fusion), channel_id=1, source_target_pairs={{0,24},{8,16},{16,8},{24,0},{1,25},{9,17},{17,9},{25,1},{2,26},{10... | collective-permute-start | bytes 1160 | tf_op jit(solution)/shard_map/ppermute | solution.py:17
  6.4 0.9 collective-permute-done.2
  7.3 2.0 collective-permute-done.1
  10.5 1.2 fusion.2
  11.6 2.7 collective-permute-start.8
  14.3 1.5 collective-permute-start.28
  15.8 1.6 collective-permute-start.6
  17.9 12.3 %collective-permute-done.8.refs_5_ = bf16[96,2048]{1,0:T(8,128)(2,1)S(1)} collective-permute-done((bf16[96,2048]{1,0:T(8,128)(2,1)S(1)}, bf16[96,2048]{1,0:T(8,128)(2,1)S(1)}, u32[]{:S(2)}, u32[]{:S(2)}) %collective-permute-start.8) | collective-permute-done | bytes 393248 | tf_op jit(solution)/shard_map/ppermute | solution.py:17
  30.3 1.5 collective-permute-start.31
  32.9 2.6 dynamic-slice_bitcast_fusion
  35.5 1.2 pad_maximum_fusion
  37.0 3.2 %collective-permute-done.31.refs_13_ = bf16[96,2048]{1,0:T(8,128)(2,1)S(1)} collective-permute-done((bf16[96,2048]{1,0:T(8,128)(2,1)S(1)}, bf16[96,2048]{1,0:T(8,128)(2,1)S(1)}, u32[]{:S(2)}, u32[]{:S(2)}) %collective-permute-start.31) | collective-permute-done | bytes 393248 | tf_op jit(solution)/shard_map/ppermute | solution.py:17
  40.2 1.5 collective-permute-start.13
  42.3 0.7 copy-done.10
  43.3 1.7 bitcast_dynamic-update-slice_fusion
  45.0 7.2 %collective-permute-done.13.refs_11_ = bf16[96,2048]{1,0:T(8,128)(2,1)S(1)} collective-permute-done((bf16[96,2048]{1,0:T(8,128)(2,1)S(1)}, bf16[96,2048]{1,0:T(8,128)(2,1)S(1)}, u32[]{:S(2)}, u32[]{:S(2)}) %collective-permute-start.13) | collective-permute-done | bytes 393248 | tf_op jit(solution)/shard_map/ppermute | solution.py:17
  52.7 1.7 collective-permute-start.4
  54.4 6.3 %collective-permute-done.19.refs_15_ = bf16[96,2048]{1,0:T(8,128)(2,1)} collective-permute-done((bf16[96,2048]{1,0:T(8,128)(2,1)}, bf16[96,2048]{1,0:T(8,128)(2,1)}, u32[]{:S(2)}, u32[]{:S(2)}) %collective-permute-start.19) | collective-permute-done | bytes 393248 | tf_op jit(solution)/shard_map/ppermute | solution.py:17
  61.2 1.6 collective-permute-start.14
  62.8 1.0 copy-done.5
  63.8 1.0 copy-done.11
  64.8 13.0 %shard_map.67 = (f32[768,2048]{1,0:T(8,128)S(1)}, bf16[1,768,2048]{2,1,0:T(8,128)(2,1)S(1)}, f32[2,8,128]{2,1,0:T(8,128)}) custom-call(s32[4]{0:T(128)S(1)} %pad_add_fusion.refs_0_, bf16[96,2048]{1,0:T(8,128)(2,1)S(1)} %bitcast.90, bf16[96,2048]{1,0:T(8,128)(2,1)S(1)} %copy-done.5, bf16[96,2048]{1,0:T(8,128)(2,1)S(1)} %collective-permute-done.6.refs_3_, ...), custom_call_target="tpu_custom_call" | custom-call | flops 6442450944 | bytes 20971520 | tf_op jit(solution)/shard_map/pallas_call | solution.py:183
  77.8 2.7 copy-done
  80.6 1.6 collective-permute-start.17
  83.1 2.0 fusion.29
  85.5 6.6 %collective-permute-done.17.refs_5_ = bf16[96,2048]{1,0:T(8,128)(2,1)S(1)} collective-permute-done((bf16[96,2048]{1,0:T(8,128)(2,1)S(1)}, bf16[96,2048]{1,0:T(8,128)(2,1)S(1)}, u32[]{:S(2)}, u32[]{:S(2)}) %collective-permute-start.17) | collective-permute-done | bytes 393248 | tf_op jit(solution)/shard_map/ppermute | solution.py:17
  92.6 1.3 collective-permute-done.20.refs_7_
  96.3 22.7 %shard_map.68 = (f32[768,2048]{1,0:T(8,128)S(1)}, bf16[2,768,2048]{2,1,0:T(8,128)(2,1)S(1)}, f32[2,8,128]{2,1,0:T(8,128)}) custom-call(s32[4]{0:T(128)S(1)} %pad_add_fusion.refs_0_, bf16[96,2048]{1,0:T(8,128)(2,1)S(1)} %collective-permute-done.3.refs_1_, bf16[96,2048]{1,0:T(8,128)(2,1)S(1)} %collective-permute-done.22.refs_2_, ...), custom_call_target="tpu_custom_call" | custom-call | flops 12884901888 | bytes 29360128 | tf_op jit(solution)/shard_map/pallas_call | solution.py:183
  119.0 4.5 %collective-permute-start.35 = (f32[2,32,2048]{2,1,0:T(8,128)S(1)}, f32[2,32,2048]{2,1,0:T(8,128)S(1)}, u32[]{:S(2)}, u32[]{:S(2)}) collective-permute-start(f32[2,32,2048]{2,1,0:T(8,128)S(1)} %get-tuple-element.55), channel_id=1, source_target_pairs={{0,2},{1,3},{2,0},{3,1},{4,6},{5,7},{6,4},{7,5},{8,10},{9,11},{10,... | collective-permute-start | bytes 1572872 | tf_op jit(solution)/shard_map/ppermute | solution.py:17
  123.7 14.9 %shard_map.69 = (f32[768,2048]{1,0:T(8,128)S(1)}, bf16[1,768,2048]{2,1,0:T(8,128)(2,1)S(1)}, f32[2,8,128]{2,1,0:T(8,128)S(1)}) custom-call(s32[4]{0:T(128)S(1)} %pad_add_fusion.refs_0_, bf16[96,2048]{1,0:T(8,128)(2,1)S(1)} %copy-done.7, bf16[96,2048]{1,0:T(8,128)(2,1)S(1)} %collective-permute-done.12.refs_2_, bf16[96,2048]{1,0:T(8,128)(2,1)S(1)} %copy-done.9, ...), custom_call_target="tpu_custom_call" | custom-call | flops 6442450944 | bytes 20971520 | tf_op jit(solution)/shard_map/pallas_call | solution.py:183
  138.5 0.8 collective-permute-start.40
  139.4 1.2 collective-permute-start.39
  140.6 1.5 collective-permute-start.38
  142.1 1.0 collective-permute-done.40.refs_3_
  143.1 1.1 collective-permute-done.38.refs_1_
  144.3 3.7 %collective-permute-start.43 = (f32[2,8,128]{2,1,0:T(8,128)S(1)}, f32[2,8,128]{2,1,0:T(8,128)S(1)}, u32[]{:S(2)}, u32[]{:S(2)}) collective-permute-start(f32[2,8,128]{2,1,0:T(8,128)S(1)} %merge.3.refs_0_), channel_id=1, source_target_pairs={{0,6},{1,7},{2,4},{3,5},{4,2},{5,3},{6,0},{7,1},{8,14},{9,15},{10,... | collective-permute-start | bytes 24584 | tf_op jit(solution)/shard_map/ppermute | solution.py:17
  148.8 1.0 collective-permute-done.43.refs_3_
  149.8 2.8 collective-permute-done.42.refs_2_
  152.8 1.1 collective-permute-done.44.refs_1_
  153.9 4.5 %delta.1 = (bf16[768,2048]{1,0:T(8,128)(2,1)S(1)}, f32[8,128]{1,0:T(8,128)S(1)}) custom-call(f32[768,2048]{1,0:T(8,128)S(1)} %get-tuple-element.54.logits_ref, f32[8,32,2048]{2,1,0:T(8,128)S(1)} %constant_dynamic-update-slice_fusion.teacher_ref, f32[8,128]{1,0:T(8,128)S(1)} %merge.5.norm_ref), custom_call_target="tpu_custom_call" | custom-call | flops 12582912 | bytes 11534336 | tf_op jit(solution)/shard_map/delta/pallas_call | solution.py:228
  158.4 9.7 %shard_map.70 = (bf16[4,96,2048]{2,1,0:T(8,128)(2,1)S(1)}, bf16[4,96,2048]{2,1,0:T(8,128)(2,1)S(1)}) custom-call(s32[4]{0:T(128)S(1)} %pad_add_fusion.refs_0_, bf16[768,2048]{1,0:T(8,128)(2,1)S(1)} %get-tuple-element.59.refs_1_.refs_2_, bf16[8192,2048]{1,0:T(8,128)(2,1)} %refs_2_.7), custom_call_target="tpu_custom_call" | custom-call | flops 6442450944 | bytes 14680064 | tf_op jit(solution)/shard_map/pallas_call | solution.py:274
  168.3 9.9 %shard_map.71 = (bf16[4,96,2048]{2,1,0:T(8,128)(2,1)S(1)}, bf16[4,96,2048]{2,1,0:T(8,128)(2,1)S(1)}) custom-call(s32[4]{0:T(128)S(1)} %pad_add_fusion.refs_0_, bf16[768,2048]{1,0:T(8,128)(2,1)S(1)} %get-tuple-element.59.refs_1_.refs_2_, bf16[8192,2048]{1,0:T(8,128)(2,1)} %refs_2_.7, bf16[4,96,2048]{2,1,0:T(8,128)(2,1)S(1)} %get-tuple-element.60.refs_3_), custom_call_target="tpu_custom_call" | custom-call | flops 6442450944 | bytes 14680064 | tf_op jit(solution)/shard_map/pallas_call | solution.py:274
  180.1 1.5 collective-permute-start.58
  181.6 1.5 collective-permute-start.53
  183.0 9.7 %shard_map.72 = (bf16[4,96,2048]{2,1,0:T(8,128)(2,1)S(1)}, bf16[4,96,2048]{2,1,0:T(8,128)(2,1)S(1)}) custom-call(s32[4]{0:T(128)S(1)} %pad_add_fusion.refs_0_, bf16[768,2048]{1,0:T(8,128)(2,1)S(1)} %get-tuple-element.59.refs_1_.refs_2_, bf16[8192,2048]{1,0:T(8,128)(2,1)} %refs_2_.7, bf16[4,96,2048]{2,1,0:T(8,128)(2,1)S(1)} %get-tuple-element.61.refs_3_, ...), custom_call_target="tpu_custom_call" | custom-call | flops 6442450944 | bytes 14680064 | tf_op jit(solution)/shard_map/pallas_call | solution.py:274
  192.8 9.7 %shard_map.73 = (bf16[4,96,2048]{2,1,0:T(8,128)(2,1)S(1)}, bf16[4,96,2048]{2,1,0:T(8,128)(2,1)S(1)}) custom-call(s32[4]{0:T(128)S(1)} %pad_add_fusion.refs_0_, bf16[768,2048]{1,0:T(8,128)(2,1)S(1)} %get-tuple-element.59.refs_1_.refs_2_, bf16[8192,2048]{1,0:T(8,128)(2,1)} %refs_2_.7, bf16[4,96,2048]{2,1,0:T(8,128)(2,1)S(1)} %get-tuple-element.63.refs_3_), custom_call_target="tpu_custom_call" | custom-call | flops 6442450944 | bytes 14680064 | tf_op jit(solution)/shard_map/pallas_call | solution.py:274
  203.7 10.4 %collective-permute-done.50 = bf16[96,2048]{1,0:T(8,128)(2,1)S(1)} collective-permute-done((bf16[96,2048]{1,0:T(8,128)(2,1)S(1)}, bf16[96,2048]{1,0:T(8,128)(2,1)S(1)}, u32[]{:S(2)}, u32[]{:S(2)}) %collective-permute-start.50) | collective-permute-done | bytes 393248 | tf_op jit(solution)/shard_map/ppermute | solution.py:17
  215.1 1.5 collective-permute-start.59
  218.8 9.6 %shard_map.74.refs_4_ = bf16[8192,2048]{1,0:T(8,128)(2,1)} custom-call(s32[4]{0:T(128)S(1)} %pad_add_fusion.refs_0_, bf16[1,768,2048]{2,1,0:T(8,128)(2,1)S(1)} %copy-done.2, bf16[768,2048]{1,0:T(8,128)(2,1)S(1)} %get-tuple-element.59.refs_1_.refs_2_, bf16[4,96,2048]{2,1,0:T(8,128)(2,1)S(1)} %get-tuple-element.64.refs_3_, ...), custom_call_target="tpu_custom_call" | custom-call | flops 6442450944 | bytes 14680064 | tf_op jit(solution)/shard_map/pallas_call | solution.py:311
  228.4 13.3 %collective-permute-done.51 = bf16[96,2048]{1,0:T(8,128)(2,1)S(1)} collective-permute-done((bf16[96,2048]{1,0:T(8,128)(2,1)S(1)}, bf16[96,2048]{1,0:T(8,128)(2,1)S(1)}, u32[]{:S(2)}, u32[]{:S(2)}) %collective-permute-start.51) | collective-permute-done | bytes 393248 | tf_op jit(solution)/shard_map/ppermute | solution.py:17
  242.2 1.5 collective-permute-start.57
  244.0 1.1 collective-permute-done.64
  245.1 9.6 %shard_map.75.refs_4_ = bf16[8192,2048]{1,0:T(8,128)(2,1)} custom-call(s32[4]{0:T(128)S(1)} %pad_add_fusion.refs_0_, bf16[2,768,2048]{2,1,0:T(8,128)(2,1)S(1)} %get-tuple-element.73.refs_1_, bf16[768,2048]{1,0:T(8,128)(2,1)S(1)} %get-tuple-element.59.refs_1_.refs_2_, bf16[96,2048]{1,0:T(8,128)(2,1)S(1)} %fusion.20.refs_3_, ...), custom_call_target="tpu_custom_call", output_to_operand_aliasing={{}: (4, {})} | custom-call | flops 6442450944 | bytes 14680064 | tf_op jit(solution)/shard_map/pallas_call | solution.py:311
  255.9 6.1 %collective-permute-done.57 = bf16[96,2048]{1,0:T(8,128)(2,1)S(1)} collective-permute-done((bf16[96,2048]{1,0:T(8,128)(2,1)S(1)}, bf16[96,2048]{1,0:T(8,128)(2,1)S(1)}, u32[]{:S(2)}, u32[]{:S(2)}) %collective-permute-start.57) | collective-permute-done | bytes 393248 | tf_op jit(solution)/shard_map/ppermute | solution.py:17
  262.6 2.1 collective-permute-start.56
  264.6 2.0 collective-permute-start.60
  266.7 9.6 %shard_map.76.refs_4_ = bf16[8192,2048]{1,0:T(8,128)(2,1)} custom-call(s32[4]{0:T(128)S(1)} %pad_add_fusion.refs_0_, bf16[2,768,2048]{2,1,0:T(8,128)(2,1)S(1)} %get-tuple-element.73.refs_1_, bf16[768,2048]{1,0:T(8,128)(2,1)S(1)} %get-tuple-element.59.refs_1_.refs_2_, bf16[96,2048]{1,0:T(8,128)(2,1)S(1)} %get-tuple-element.82.refs_3_, ...), custom_call_target="tpu_custom_call", output_to_operand_aliasing={{}: (4, {})} | custom-call | flops 6442450944 | bytes 14680064 | tf_op jit(solution)/shard_map/pallas_call | solution.py:311
  276.3 1.0 collective-permute-start.66
  277.2 3.6 %collective-permute-done.66 = f32[1,8]{1,0:T(1,128)S(1)} collective-permute-done((f32[1,8]{1,0:T(1,128)S(1)}, f32[1,8]{1,0:T(1,128)S(1)}, u32[]{:S(2)}, u32[]{:S(2)}) %collective-permute-start.66) | collective-permute-done | bytes 64 | tf_op jit(solution)/shard_map/ppermute | solution.py:17
  281.5 2.0 collective-permute-start.69
  283.5 1.5 collective-permute-start.67
  285.0 9.6 %shard_map.77 = bf16[8192,2048]{1,0:T(8,128)(2,1)} custom-call(s32[4]{0:T(128)S(1)} %pad_add_fusion.refs_0_, bf16[1,768,2048]{2,1,0:T(8,128)(2,1)S(1)} %get-tuple-element.72.refs_1_, bf16[768,2048]{1,0:T(8,128)(2,1)S(1)} %get-tuple-element.59.refs_1_.refs_2_, bf16[96,2048]{1,0:T(8,128)(2,1)S(1)} %get-tuple-element.81.refs_3_, ...), custom_call_target="tpu_custom_call", output_to_operand_aliasing={{}: (4, {})} | custom-call | flops 6442450944 | bytes 14680064 | tf_op jit(solution)/shard_map/pallas_call | solution.py:311
  295.1 1.1 fusion.7
  (159 shorter events, 21.1 us)
Async XLA Ops:
  1.8 5.5 %collective-permute-start.2 = (f32[3,32]{1,0:T(4,128)S(1)}, f32[3,32]{1,0:T(4,128)S(1)}, u32[]{:S(2)}, u32[]{:S(2)}) collective-permute-start(f32[3,32]{1,0:T(4,128)S(1)} %fusion), channel_id=1, source_target_pairs={{0,24},{8,16},{16,8},{24,0},{1,25},{9,17},{17,9},{25,1},{2,26},{10... | collective-permute-start | bytes 1160 | tf_op jit(solution)/shard_map/ppermute | solution.py:17
  5.8 3.6 %collective-permute-start.1 = (f32[3,32]{1,0:T(4,128)S(1)}, f32[3,32]{1,0:T(4,128)S(1)}, u32[]{:S(2)}, u32[]{:S(2)}) collective-permute-start(f32[3,32]{1,0:T(4,128)S(1)} %fusion), channel_id=1, source_target_pairs={{0,16},{8,24},{16,0},{24,8},{1,17},{9,25},{17,1},{25,9},{2,18},{10... | collective-permute-start | bytes 1160 | tf_op jit(solution)/shard_map/ppermute | solution.py:17
  6.3 3.6 %collective-permute-start = (f32[3,32]{1,0:T(4,128)S(1)}, f32[3,32]{1,0:T(4,128)S(1)}, u32[]{:S(2)}, u32[]{:S(2)}) collective-permute-start(f32[3,32]{1,0:T(4,128)S(1)} %fusion), channel_id=1, source_target_pairs={{0,8},{8,0},{16,24},{24,16},{1,9},{9,1},{17,25},{25,17},{2,10},{10... | collective-permute-start | bytes 1160 | tf_op jit(solution)/shard_map/ppermute | solution.py:17
  11.6 18.6 %collective-permute-start.8 = (bf16[96,2048]{1,0:T(8,128)(2,1)S(1)}, bf16[96,2048]{1,0:T(8,128)(2,1)S(1)}, u32[]{:S(2)}, u32[]{:S(2)}) collective-permute-start(bf16[96,2048]{1,0:T(8,128)(2,1)S(1)} %bitcast.85), channel_id=1, source_target_pairs={{0,4},{1,5},{2,6},{3,7},{4,0},{5,1},{6,2},{7,3},{8,12},{9,13},{10,... | collective-permute-start | bytes 1179656 | tf_op jit(solution)/shard_map/ppermute | solution.py:17
  14.3 17.5 %collective-permute-start.28 = (bf16[96,2048]{1,0:T(8,128)(2,1)S(1)}, bf16[96,2048]{1,0:T(8,128)(2,1)S(1)}, u32[]{:S(2)}, u32[]{:S(2)}) collective-permute-start(bf16[96,2048]{1,0:T(8,128)(2,1)S(1)} %bitcast.86), channel_id=1, source_target_pairs={{0,16},{8,24},{16,0},{24,8},{1,17},{9,25},{17,1},{25,9},{2,18},{10... | collective-permute-start | bytes 1179656 | tf_op jit(solution)/shard_map/ppermute | solution.py:17
  15.8 16.6 %collective-permute-start.6 = (bf16[96,2048]{1,0:T(8,128)(2,1)S(1)}, bf16[96,2048]{1,0:T(8,128)(2,1)S(1)}, u32[]{:S(2)}, u32[]{:S(2)}) collective-permute-start(bf16[96,2048]{1,0:T(8,128)(2,1)S(1)} %bitcast.87), channel_id=1, source_target_pairs={{0,2},{1,3},{2,0},{3,1},{4,6},{5,7},{6,4},{7,5},{8,10},{9,11},{10,... | collective-permute-start | bytes 1179656 | tf_op jit(solution)/shard_map/ppermute | solution.py:17
  17.4 15.5 %collective-permute-start.5 = (bf16[96,2048]{1,0:T(8,128)(2,1)S(1)}, bf16[96,2048]{1,0:T(8,128)(2,1)S(1)}, u32[]{:S(2)}, u32[]{:S(2)}) collective-permute-start(bf16[96,2048]{1,0:T(8,128)(2,1)S(1)} %bitcast.88), channel_id=1, source_target_pairs={{0,1},{1,0},{2,3},{3,2},{4,5},{5,4},{6,7},{7,6},{8,9},{9,8},{10,11... | collective-permute-start | bytes 1179656 | tf_op jit(solution)/shard_map/ppermute | solution.py:17
  17.4 19.3 %collective-permute-start.3 = (bf16[96,2048]{1,0:T(8,128)(2,1)S(1)}, bf16[96,2048]{1,0:T(8,128)(2,1)S(1)}, u32[]{:S(2)}, u32[]{:S(2)}) collective-permute-start(bf16[96,2048]{1,0:T(8,128)(2,1)S(1)} %bitcast.89), channel_id=1, source_target_pairs={{0,8},{8,0},{16,24},{24,16},{1,9},{9,1},{17,25},{25,17},{2,10},{10... | collective-permute-start | bytes 1179656 | tf_op jit(solution)/shard_map/ppermute | solution.py:17
  30.3 10.0 %collective-permute-start.31 = (bf16[96,2048]{1,0:T(8,128)(2,1)S(1)}, bf16[96,2048]{1,0:T(8,128)(2,1)S(1)}, u32[]{:S(2)}, u32[]{:S(2)}) collective-permute-start(bf16[96,2048]{1,0:T(8,128)(2,1)S(1)} %collective-permute-done.8.refs_5_), channel_id=1, source_target_pairs={{0,16},{8,24},{16,0},{24,8},{1,17},{9,25},{17,1},{25,9},{2,18},{10... | collective-permute-start | bytes 1179656 | tf_op jit(solution)/shard_map/ppermute | solution.py:17
  31.8 10.0 %collective-permute-start.16 = (bf16[96,2048]{1,0:T(8,128)(2,1)S(1)}, bf16[96,2048]{1,0:T(8,128)(2,1)S(1)}, u32[]{:S(2)}, u32[]{:S(2)}) collective-permute-start(bf16[96,2048]{1,0:T(8,128)(2,1)S(1)} %collective-permute-done.8.refs_5_), channel_id=1, source_target_pairs={{0,8},{8,0},{16,24},{24,16},{1,9},{9,1},{17,25},{25,17},{2,10},{10... | collective-permute-start | bytes 1179656 | tf_op jit(solution)/shard_map/ppermute | solution.py:17
  32.4 9.6 %collective-permute-start.10 = (bf16[96,2048]{1,0:T(8,128)(2,1)S(1)}, bf16[96,2048]{1,0:T(8,128)(2,1)}, u32[]{:S(2)}, u32[]{:S(2)}) collective-permute-start(bf16[96,2048]{1,0:T(8,128)(2,1)S(1)} %collective-permute-done.8.refs_5_), channel_id=1, source_target_pairs={{0,2},{1,3},{2,0},{3,1},{4,6},{5,7},{6,4},{7,5},{8,10},{9,11},{10,... | collective-permute-start | bytes 1179656 | tf_op jit(solution)/shard_map/ppermute | solution.py:17
  32.9 9.4 %collective-permute-start.9 = (bf16[96,2048]{1,0:T(8,128)(2,1)S(1)}, bf16[96,2048]{1,0:T(8,128)(2,1)S(1)}, u32[]{:S(2)}, u32[]{:S(2)}) collective-permute-start(bf16[96,2048]{1,0:T(8,128)(2,1)S(1)} %collective-permute-done.8.refs_5_), channel_id=1, source_target_pairs={{0,1},{1,0},{2,3},{3,2},{4,5},{5,4},{6,7},{7,6},{8,9},{9,8},{10,11... | collective-permute-start | bytes 1179656 | tf_op jit(solution)/shard_map/ppermute | solution.py:17
  36.7 45.5 %collective-permute-start.34 = (f32[4,32,2048]{2,1,0:T(8,128)}, f32[4,32,2048]{2,1,0:T(8,128)}, u32[]{:S(2)}, u32[]{:S(2)}) collective-permute-start(f32[4,32,2048]{2,1,0:T(8,128)} %pad_maximum_fusion), channel_id=1, source_target_pairs={{0,1},{1,0},{2,3},{3,2},{4,5},{5,4},{6,7},{7,6},{8,9},{9,8},{10,11... | collective-permute-start | bytes 3145736 | tf_op jit(solution)/shard_map/ppermute | solution.py:17
  40.2 12.0 %collective-permute-start.13 = (bf16[96,2048]{1,0:T(8,128)(2,1)S(1)}, bf16[96,2048]{1,0:T(8,128)(2,1)S(1)}, u32[]{:S(2)}, u32[]{:S(2)}) collective-permute-start(bf16[96,2048]{1,0:T(8,128)(2,1)S(1)} %collective-permute-done.6.refs_3_), channel_id=1, source_target_pairs={{0,16},{8,24},{16,0},{24,8},{1,17},{9,25},{17,1},{25,9},{2,18},{10... | collective-permute-start | bytes 1179656 | tf_op jit(solution)/shard_map/ppermute | solution.py:17
  41.8 10.9 %collective-permute-start.7 = (bf16[96,2048]{1,0:T(8,128)(2,1)S(1)}, bf16[96,2048]{1,0:T(8,128)(2,1)}, u32[]{:S(2)}, u32[]{:S(2)}) collective-permute-start(bf16[96,2048]{1,0:T(8,128)(2,1)S(1)} %collective-permute-done.6.refs_3_), channel_id=1, source_target_pairs={{0,1},{1,0},{2,3},{3,2},{4,5},{5,4},{6,7},{7,6},{8,9},{9,8},{10,11... | collective-permute-start | bytes 1179656 | tf_op jit(solution)/shard_map/ppermute | solution.py:17
  42.0 18.8 %collective-permute-start.19 = (bf16[96,2048]{1,0:T(8,128)(2,1)}, bf16[96,2048]{1,0:T(8,128)(2,1)}, u32[]{:S(2)}, u32[]{:S(2)}) collective-permute-start(bf16[96,2048]{1,0:T(8,128)(2,1)} %collective-permute-done.10.refs_7_), channel_id=1, source_target_pairs={{0,16},{8,24},{16,0},{24,8},{1,17},{9,25},{17,1},{25,9},{2,18},{10... | collective-permute-start | bytes 1179656 | tf_op jit(solution)/shard_map/ppermute | solution.py:17
  43.1 18.1 %collective-permute-start.11 = (bf16[96,2048]{1,0:T(8,128)(2,1)}, bf16[96,2048]{1,0:T(8,128)(2,1)}, u32[]{:S(2)}, u32[]{:S(2)}) collective-permute-start(bf16[96,2048]{1,0:T(8,128)(2,1)} %collective-permute-done.10.refs_7_), channel_id=1, source_target_pairs={{0,1},{1,0},{2,3},{3,2},{4,5},{5,4},{6,7},{7,6},{8,9},{9,8},{10,11... | collective-permute-start | bytes 1179656 | tf_op jit(solution)/shard_map/ppermute | solution.py:17
  52.2 28.2 %collective-permute-start.23 = (bf16[96,2048]{1,0:T(8,128)(2,1)S(1)}, bf16[96,2048]{1,0:T(8,128)(2,1)S(1)}, u32[]{:S(2)}, u32[]{:S(2)}) collective-permute-start(bf16[96,2048]{1,0:T(8,128)(2,1)S(1)} %collective-permute-done.6.refs_3_), channel_id=1, source_target_pairs={{0,8},{8,0},{16,24},{24,16},{1,9},{9,1},{17,25},{25,17},{2,10},{10... | collective-permute-start | bytes 1179656 | tf_op jit(solution)/shard_map/ppermute | solution.py:17
  52.7 27.9 %collective-permute-start.4 = (bf16[96,2048]{1,0:T(8,128)(2,1)S(1)}, bf16[96,2048]{1,0:T(8,128)(2,1)S(1)}, u32[]{:S(2)}, u32[]{:S(2)}) collective-permute-start(bf16[96,2048]{1,0:T(8,128)(2,1)S(1)} %collective-permute-done.3.refs_1_), channel_id=1, source_target_pairs={{0,16},{8,24},{16,0},{24,8},{1,17},{9,25},{17,1},{25,9},{2,18},{10... | collective-permute-start | bytes 1179656 | tf_op jit(solution)/shard_map/ppermute | solution.py:17
  60.8 21.5 %collective-permute-start.26 = (bf16[96,2048]{1,0:T(8,128)(2,1)}, bf16[96,2048]{1,0:T(8,128)(2,1)S(1)}, u32[]{:S(2)}, u32[]{:S(2)}) collective-permute-start(bf16[96,2048]{1,0:T(8,128)(2,1)} %collective-permute-done.10.refs_7_), channel_id=1, source_target_pairs={{0,8},{8,0},{16,24},{24,16},{1,9},{9,1},{17,25},{25,17},{2,10},{10... | collective-permute-start | bytes 1179656 | tf_op jit(solution)/shard_map/ppermute | solution.py:17
  61.2 21.8 %collective-permute-start.14 = (bf16[96,2048]{1,0:T(8,128)(2,1)S(1)}, bf16[96,2048]{1,0:T(8,128)(2,1)S(1)}, u32[]{:S(2)}, u32[]{:S(2)}) collective-permute-start(bf16[96,2048]{1,0:T(8,128)(2,1)S(1)} %collective-permute-done.13.refs_11_), channel_id=1, source_target_pairs={{0,8},{8,0},{16,24},{24,16},{1,9},{9,1},{17,25},{25,17},{2,10},{10... | collective-permute-start | bytes 1179656 | tf_op jit(solution)/shard_map/ppermute | solution.py:17
  80.5 4.7 %collective-permute-start.25 = (bf16[96,2048]{1,0:T(8,128)(2,1)S(1)}, bf16[96,2048]{1,0:T(8,128)(2,1)S(1)}, u32[]{:S(2)}, u32[]{:S(2)}) collective-permute-start(bf16[96,2048]{1,0:T(8,128)(2,1)S(1)} %collective-permute-done.16.refs_5_), channel_id=1, source_target_pairs={{0,1},{1,0},{2,3},{3,2},{4,5},{5,4},{6,7},{7,6},{8,9},{9,8},{10,11... | collective-permute-start | bytes 1179656 | tf_op jit(solution)/shard_map/ppermute | solution.py:17
  80.6 11.5 %collective-permute-start.17 = (bf16[96,2048]{1,0:T(8,128)(2,1)S(1)}, bf16[96,2048]{1,0:T(8,128)(2,1)S(1)}, u32[]{:S(2)}, u32[]{:S(2)}) collective-permute-start(bf16[96,2048]{1,0:T(8,128)(2,1)S(1)} %collective-permute-done.16.refs_5_), channel_id=1, source_target_pairs={{0,16},{8,24},{16,0},{24,8},{1,17},{9,25},{17,1},{25,9},{2,18},{10... | collective-permute-start | bytes 1179656 | tf_op jit(solution)/shard_map/ppermute | solution.py:17
  82.2 9.9 %collective-permute-start.33 = (bf16[96,2048]{1,0:T(8,128)(2,1)}, bf16[96,2048]{1,0:T(8,128)(2,1)S(1)}, u32[]{:S(2)}, u32[]{:S(2)}) collective-permute-start(bf16[96,2048]{1,0:T(8,128)(2,1)} %collective-permute-done.19.refs_15_), channel_id=1, source_target_pairs={{0,1},{1,0},{2,3},{3,2},{4,5},{5,4},{6,7},{7,6},{8,9},{9,8},{10,11... | collective-permute-start | bytes 1179656 | tf_op jit(solution)/shard_map/ppermute | solution.py:17
  82.3 11.6 %collective-permute-start.20 = (bf16[96,2048]{1,0:T(8,128)(2,1)}, bf16[96,2048]{1,0:T(8,128)(2,1)S(1)}, u32[]{:S(2)}, u32[]{:S(2)}) collective-permute-start(bf16[96,2048]{1,0:T(8,128)(2,1)} %collective-permute-done.19.refs_15_), channel_id=1, source_target_pairs={{0,8},{8,0},{16,24},{24,16},{1,9},{9,1},{17,25},{25,17},{2,10},{10... | collective-permute-start | bytes 1179656 | tf_op jit(solution)/shard_map/ppermute | solution.py:17
  83.0 10.9 %collective-permute-start.22 = (bf16[96,2048]{1,0:T(8,128)(2,1)S(1)}, bf16[96,2048]{1,0:T(8,128)(2,1)S(1)}, u32[]{:S(2)}, u32[]{:S(2)}) collective-permute-start(bf16[96,2048]{1,0:T(8,128)(2,1)S(1)} %collective-permute-done.3.refs_1_), channel_id=1, source_target_pairs={{0,1},{1,0},{2,3},{3,2},{4,5},{5,4},{6,7},{7,6},{8,9},{9,8},{10,11... | collective-permute-start | bytes 1179656 | tf_op jit(solution)/shard_map/ppermute | solution.py:17
  85.1 9.5 %collective-permute-start.24 = (bf16[96,2048]{1,0:T(8,128)(2,1)S(1)}, bf16[96,2048]{1,0:T(8,128)(2,1)S(1)}, u32[]{:S(2)}, u32[]{:S(2)}) collective-permute-start(bf16[96,2048]{1,0:T(8,128)(2,1)S(1)} %collective-permute-done.23.refs_3_), channel_id=1, source_target_pairs={{0,1},{1,0},{2,3},{3,2},{4,5},{5,4},{6,7},{7,6},{8,9},{9,8},{10,11... | collective-permute-start | bytes 1179656 | tf_op jit(solution)/shard_map/ppermute | solution.py:17
  94.6 54.1 %collective-permute-start.36 = (f32[2,32,2048]{2,1,0:T(8,128)S(1)}, f32[2,32,2048]{2,1,0:T(8,128)S(1)}, u32[]{:S(2)}, u32[]{:S(2)}) collective-permute-start(f32[2,32,2048]{2,1,0:T(8,128)S(1)} %get-tuple-element.56), channel_id=1, source_target_pairs={{0,4},{1,5},{2,6},{3,7},{4,0},{5,1},{6,2},{7,3},{8,12},{9,13},{10,... | collective-permute-start | bytes 1572872 | tf_op jit(solution)/shard_map/ppermute | solution.py:17
  94.7 24.3 %collective-permute-start.12 = (bf16[96,2048]{1,0:T(8,128)(2,1)S(1)}, bf16[96,2048]{1,0:T(8,128)(2,1)S(1)}, u32[]{:S(2)}, u32[]{:S(2)}) collective-permute-start(bf16[96,2048]{1,0:T(8,128)(2,1)S(1)} %collective-permute-done.4.refs_1_), channel_id=1, source_target_pairs={{0,1},{1,0},{2,3},{3,2},{4,5},{5,4},{6,7},{7,6},{8,9},{9,8},{10,11... | collective-permute-start | bytes 1179656 | tf_op jit(solution)/shard_map/ppermute | solution.py:17
  94.8 28.7 %collective-permute-start.15 = (bf16[96,2048]{1,0:T(8,128)(2,1)S(1)}, bf16[96,2048]{1,0:T(8,128)(2,1)S(1)}, u32[]{:S(2)}, u32[]{:S(2)}) collective-permute-start(bf16[96,2048]{1,0:T(8,128)(2,1)S(1)} %collective-permute-done.14.refs_3_), channel_id=1, source_target_pairs={{0,1},{1,0},{2,3},{3,2},{4,5},{5,4},{6,7},{7,6},{8,9},{9,8},{10,11... | collective-permute-start | bytes 1179656 | tf_op jit(solution)/shard_map/ppermute | solution.py:17
  95.6 28.0 %collective-permute-start.18 = (bf16[96,2048]{1,0:T(8,128)(2,1)S(1)}, bf16[96,2048]{1,0:T(8,128)(2,1)S(1)}, u32[]{:S(2)}, u32[]{:S(2)}) collective-permute-start(bf16[96,2048]{1,0:T(8,128)(2,1)S(1)} %collective-permute-done.17.refs_5_), channel_id=1, source_target_pairs={{0,1},{1,0},{2,3},{3,2},{4,5},{5,4},{6,7},{7,6},{8,9},{9,8},{10,11... | collective-permute-start | bytes 1179656 | tf_op jit(solution)/shard_map/ppermute | solution.py:17
  96.2 27.4 %collective-permute-start.21 = (bf16[96,2048]{1,0:T(8,128)(2,1)S(1)}, bf16[96,2048]{1,0:T(8,128)(2,1)S(1)}, u32[]{:S(2)}, u32[]{:S(2)}) collective-permute-start(bf16[96,2048]{1,0:T(8,128)(2,1)S(1)} %collective-permute-done.20.refs_7_), channel_id=1, source_target_pairs={{0,1},{1,0},{2,3},{3,2},{4,5},{5,4},{6,7},{7,6},{8,9},{9,8},{10,11... | collective-permute-start | bytes 1179656 | tf_op jit(solution)/shard_map/ppermute | solution.py:17
  119.0 21.6 %collective-permute-start.35 = (f32[2,32,2048]{2,1,0:T(8,128)S(1)}, f32[2,32,2048]{2,1,0:T(8,128)S(1)}, u32[]{:S(2)}, u32[]{:S(2)}) collective-permute-start(f32[2,32,2048]{2,1,0:T(8,128)S(1)} %get-tuple-element.55), channel_id=1, source_target_pairs={{0,2},{1,3},{2,0},{3,1},{4,6},{5,7},{6,4},{7,5},{8,10},{9,11},{10,... | collective-permute-start | bytes 1572872 | tf_op jit(solution)/shard_map/ppermute | solution.py:17
  123.5 29.2 %collective-permute-start.37 = (f32[2,32,2048]{2,1,0:T(8,128)S(1)}, f32[2,32,2048]{2,1,0:T(8,128)S(1)}, u32[]{:S(2)}, u32[]{:S(2)}) collective-permute-start(f32[2,32,2048]{2,1,0:T(8,128)S(1)} %pad_maximum_fusion.3), channel_id=1, source_target_pairs={{0,6},{1,7},{2,4},{3,5},{4,2},{5,3},{6,0},{7,1},{8,14},{9,15},{10,... | collective-permute-start | bytes 1572872 | tf_op jit(solution)/shard_map/ppermute | solution.py:17
  138.5 4.6 %collective-permute-start.40 = (f32[2,8,128]{2,1,0:T(8,128)S(1)}, f32[2,8,128]{2,1,0:T(8,128)S(1)}, u32[]{:S(2)}, u32[]{:S(2)}) collective-permute-start(f32[2,8,128]{2,1,0:T(8,128)S(1)} %get-tuple-element.58.refs_0_), channel_id=1, source_target_pairs={{0,24},{8,16},{16,8},{24,0},{1,25},{9,17},{17,9},{25,1},{2,26},{10... | collective-permute-start | bytes 24584 | tf_op jit(solution)/shard_map/ppermute | solution.py:17
  139.4 3.8 %collective-permute-start.39 = (f32[2,8,128]{2,1,0:T(8,128)S(1)}, f32[2,8,128]{2,1,0:T(8,128)S(1)}, u32[]{:S(2)}, u32[]{:S(2)}) collective-permute-start(f32[2,8,128]{2,1,0:T(8,128)S(1)} %get-tuple-element.58.refs_0_), channel_id=1, source_target_pairs={{0,16},{8,24},{16,0},{24,8},{1,17},{9,25},{17,1},{25,9},{2,18},{10... | collective-permute-start | bytes 24584 | tf_op jit(solution)/shard_map/ppermute | solution.py:17
  140.6 3.7 %collective-permute-start.38 = (f32[2,8,128]{2,1,0:T(8,128)S(1)}, f32[2,8,128]{2,1,0:T(8,128)S(1)}, u32[]{:S(2)}, u32[]{:S(2)}) collective-permute-start(f32[2,8,128]{2,1,0:T(8,128)S(1)} %get-tuple-element.58.refs_0_), channel_id=1, source_target_pairs={{0,8},{8,0},{16,24},{24,16},{1,9},{9,1},{17,25},{25,17},{2,10},{10... | collective-permute-start | bytes 24584 | tf_op jit(solution)/shard_map/ppermute | solution.py:17
  144.3 5.5 %collective-permute-start.43 = (f32[2,8,128]{2,1,0:T(8,128)S(1)}, f32[2,8,128]{2,1,0:T(8,128)S(1)}, u32[]{:S(2)}, u32[]{:S(2)}) collective-permute-start(f32[2,8,128]{2,1,0:T(8,128)S(1)} %merge.3.refs_0_), channel_id=1, source_target_pairs={{0,6},{1,7},{2,4},{3,5},{4,2},{5,3},{6,0},{7,1},{8,14},{9,15},{10,... | collective-permute-start | bytes 24584 | tf_op jit(solution)/shard_map/ppermute | solution.py:17
  148.0 4.5 %collective-permute-start.42 = (f32[2,8,128]{2,1,0:T(8,128)S(1)}, f32[2,8,128]{2,1,0:T(8,128)S(1)}, u32[]{:S(2)}, u32[]{:S(2)}) collective-permute-start(f32[2,8,128]{2,1,0:T(8,128)S(1)} %merge.3.refs_0_), channel_id=1, source_target_pairs={{0,4},{1,5},{2,6},{3,7},{4,0},{5,1},{6,2},{7,3},{8,12},{9,13},{10,... | collective-permute-start | bytes 24584 | tf_op jit(solution)/shard_map/ppermute | solution.py:17
  148.0 4.5 %collective-permute-start.41 = (f32[2,8,128]{2,1,0:T(8,128)S(1)}, f32[2,8,128]{2,1,0:T(8,128)S(1)}, u32[]{:S(2)}, u32[]{:S(2)}) collective-permute-start(f32[2,8,128]{2,1,0:T(8,128)S(1)} %merge.3.refs_0_), channel_id=1, source_target_pairs={{0,2},{1,3},{2,0},{3,1},{4,6},{5,7},{6,4},{7,5},{8,10},{9,11},{10,... | collective-permute-start | bytes 24584 | tf_op jit(solution)/shard_map/ppermute | solution.py:17
  168.1 10.7 %collective-permute-start.45 = (bf16[4,96,2048]{2,1,0:T(8,128)(2,1)S(1)}, bf16[4,96,2048]{2,1,0:T(8,128)(2,1)S(1)}, u32[]{:S(2)}, u32[]{:S(2)}) collective-permute-start(bf16[4,96,2048]{2,1,0:T(8,128)(2,1)S(1)} %get-tuple-element.62), channel_id=1, source_target_pairs={{0,1},{1,0},{2,3},{3,2},{4,5},{5,4},{6,7},{7,6},{8,9},{9,8},{10,11... | collective-permute-start | bytes 4718600 | tf_op jit(solution)/shard_map/ppermute | solution.py:17
  178.2 24.3 %collective-permute-start.49 = (bf16[4,96,2048]{2,1,0:T(8,128)(2,1)S(1)}, bf16[4,96,2048]{2,1,0:T(8,128)(2,1)S(1)}, u32[]{:S(2)}, u32[]{:S(2)}) collective-permute-start(bf16[4,96,2048]{2,1,0:T(8,128)(2,1)S(1)} %get-tuple-element.67), channel_id=1, source_target_pairs={{0,1},{1,0},{2,3},{3,2},{4,5},{5,4},{6,7},{7,6},{8,9},{9,8},{10,11... | collective-permute-start | bytes 4718600 | tf_op jit(solution)/shard_map/ppermute | solution.py:17
  179.4 37.5 %collective-permute-start.61 = (bf16[96,2048]{1,0:T(8,128)(2,1)S(1)}, bf16[96,2048]{1,0:T(8,128)(2,1)S(1)}, u32[]{:S(2)}, u32[]{:S(2)}) collective-permute-start(bf16[96,2048]{1,0:T(8,128)(2,1)S(1)} %get-tuple-element.87.refs_7_), channel_id=1, source_target_pairs={{0,16},{8,24},{16,0},{24,8},{1,17},{9,25},{17,1},{25,9},{2,18},{10... | collective-permute-start | bytes 1179656 | tf_op jit(solution)/shard_map/ppermute | solution.py:17
  180.1 23.3 %collective-permute-start.58 = (bf16[96,2048]{1,0:T(8,128)(2,1)S(1)}, bf16[96,2048]{1,0:T(8,128)(2,1)S(1)}, u32[]{:S(2)}, u32[]{:S(2)}) collective-permute-start(bf16[96,2048]{1,0:T(8,128)(2,1)S(1)} %get-tuple-element.88.refs_6_), channel_id=1, source_target_pairs={{0,8},{8,0},{16,24},{24,16},{1,9},{9,1},{17,25},{25,17},{2,10},{10... | collective-permute-start | bytes 1179656 | tf_op jit(solution)/shard_map/ppermute | solution.py:17
  181.6 36.0 %collective-permute-start.53 = (bf16[96,2048]{1,0:T(8,128)(2,1)S(1)}, bf16[96,2048]{1,0:T(8,128)(2,1)S(1)}, u32[]{:S(2)}, u32[]{:S(2)}) collective-permute-start(bf16[96,2048]{1,0:T(8,128)(2,1)S(1)} %get-tuple-element.89.refs_5_), channel_id=1, source_target_pairs={{0,16},{8,24},{16,0},{24,8},{1,17},{9,25},{17,1},{25,9},{2,18},{10... | collective-permute-start | bytes 1179656 | tf_op jit(solution)/shard_map/ppermute | solution.py:17
  192.7 22.3 %collective-permute-start.47 = (bf16[4,96,2048]{2,1,0:T(8,128)(2,1)S(1)}, bf16[4,96,2048]{2,1,0:T(8,128)(2,1)S(1)}, u32[]{:S(2)}, u32[]{:S(2)}) collective-permute-start(bf16[4,96,2048]{2,1,0:T(8,128)(2,1)S(1)} %get-tuple-element.66), channel_id=1, source_target_pairs={{0,1},{1,0},{2,3},{3,2},{4,5},{5,4},{6,7},{7,6},{8,9},{9,8},{10,11... | collective-permute-start | bytes 4718600 | tf_op jit(solution)/shard_map/ppermute | solution.py:17
  202.5 11.6 %collective-permute-start.50 = (bf16[96,2048]{1,0:T(8,128)(2,1)S(1)}, bf16[96,2048]{1,0:T(8,128)(2,1)S(1)}, u32[]{:S(2)}, u32[]{:S(2)}) collective-permute-start(bf16[96,2048]{1,0:T(8,128)(2,1)S(1)} %get-tuple-element.90.refs_4_), channel_id=1, source_target_pairs={{0,8},{8,0},{16,24},{24,16},{1,9},{9,1},{17,25},{25,17},{2,10},{10... | collective-permute-start | bytes 1179656 | tf_op jit(solution)/shard_map/ppermute | solution.py:17
  203.4 38.8 %collective-permute-start.46 = (bf16[4,96,2048]{2,1,0:T(8,128)(2,1)S(1)}, bf16[4,96,2048]{2,1,0:T(8,128)(2,1)S(1)}, u32[]{:S(2)}, u32[]{:S(2)}) collective-permute-start(bf16[4,96,2048]{2,1,0:T(8,128)(2,1)S(1)} %get-tuple-element.65), channel_id=1, source_target_pairs={{0,1},{1,0},{2,3},{3,2},{4,5},{5,4},{6,7},{7,6},{8,9},{9,8},{10,11... | collective-permute-start | bytes 4718600 | tf_op jit(solution)/shard_map/ppermute | solution.py:17
  214.1 40.6 %collective-permute-start.55 = (bf16[96,2048]{1,0:T(8,128)(2,1)S(1)}, bf16[96,2048]{1,0:T(8,128)(2,1)S(1)}, u32[]{:S(2)}, u32[]{:S(2)}) collective-permute-start(bf16[96,2048]{1,0:T(8,128)(2,1)S(1)} %get-tuple-element.80.refs_7_), channel_id=1, source_target_pairs={{0,16},{8,24},{16,0},{24,8},{1,17},{9,25},{17,1},{25,9},{2,18},{10... | collective-permute-start | bytes 1179656 | tf_op jit(solution)/shard_map/ppermute | solution.py:17
  215.1 40.3 %collective-permute-start.59 = (bf16[96,2048]{1,0:T(8,128)(2,1)S(1)}, bf16[96,2048]{1,0:T(8,128)(2,1)S(1)}, u32[]{:S(2)}, u32[]{:S(2)}) collective-permute-start(bf16[96,2048]{1,0:T(8,128)(2,1)S(1)} %get-tuple-element.85.refs_9_), channel_id=1, source_target_pairs={{0,16},{8,24},{16,0},{24,8},{1,17},{9,25},{17,1},{25,9},{2,18},{10... | collective-permute-start | bytes 1179656 | tf_op jit(solution)/shard_map/ppermute | solution.py:17
  216.9 24.7 %collective-permute-start.51 = (bf16[96,2048]{1,0:T(8,128)(2,1)S(1)}, bf16[96,2048]{1,0:T(8,128)(2,1)S(1)}, u32[]{:S(2)}, u32[]{:S(2)}) collective-permute-start(bf16[96,2048]{1,0:T(8,128)(2,1)S(1)} %get-tuple-element.86.refs_5_), channel_id=1, source_target_pairs={{0,16},{8,24},{16,0},{24,8},{1,17},{9,25},{17,1},{25,9},{2,18},{10... | collective-permute-start | bytes 1179656 | tf_op jit(solution)/shard_map/ppermute | solution.py:17
  217.5 26.1 %collective-permute-start.48 = (bf16[96,2048]{1,0:T(8,128)(2,1)S(1)}, bf16[96,2048]{1,0:T(8,128)(2,1)S(1)}, u32[]{:S(2)}, u32[]{:S(2)}) collective-permute-start(bf16[96,2048]{1,0:T(8,128)(2,1)S(1)} %get-tuple-element.84.refs_4_), channel_id=1, source_target_pairs={{0,8},{8,0},{16,24},{24,16},{1,9},{9,1},{17,25},{25,17},{2,10},{10... | collective-permute-start | bytes 1179656 | tf_op jit(solution)/shard_map/ppermute | solution.py:17
  241.6 14.2 %collective-permute-start.54 = (bf16[96,2048]{1,0:T(8,128)(2,1)S(1)}, bf16[96,2048]{1,0:T(8,128)(2,1)S(1)}, u32[]{:S(2)}, u32[]{:S(2)}) collective-permute-start(bf16[96,2048]{1,0:T(8,128)(2,1)S(1)} %get-tuple-element.78.refs_6_), channel_id=1, source_target_pairs={{0,8},{8,0},{16,24},{24,16},{1,9},{9,1},{17,25},{25,17},{2,10},{10... | collective-permute-start | bytes 1179656 | tf_op jit(solution)/shard_map/ppermute | solution.py:17
  242.2 19.8 %collective-permute-start.57 = (bf16[96,2048]{1,0:T(8,128)(2,1)S(1)}, bf16[96,2048]{1,0:T(8,128)(2,1)S(1)}, u32[]{:S(2)}, u32[]{:S(2)}) collective-permute-start(bf16[96,2048]{1,0:T(8,128)(2,1)S(1)} %get-tuple-element.83.refs_8_), channel_id=1, source_target_pairs={{0,8},{8,0},{16,24},{24,16},{1,9},{9,1},{17,25},{25,17},{2,10},{10... | collective-permute-start | bytes 1179656 | tf_op jit(solution)/shard_map/ppermute | solution.py:17
  245.1 16.8 %collective-permute-start.52 = (bf16[96,2048]{1,0:T(8,128)(2,1)S(1)}, bf16[96,2048]{1,0:T(8,128)(2,1)S(1)}, u32[]{:S(2)}, u32[]{:S(2)}) collective-permute-start(bf16[96,2048]{1,0:T(8,128)(2,1)S(1)} %fusion.20.refs_3_), channel_id=1, source_target_pairs={{0,2},{1,3},{2,0},{3,1},{4,6},{5,7},{6,4},{7,5},{8,10},{9,11},{10,... | collective-permute-start | bytes 1179656 | tf_op jit(solution)/shard_map/ppermute | solution.py:17
  254.7 26.1 %collective-permute-start.63 = (bf16[96,2048]{1,0:T(8,128)(2,1)S(1)}, bf16[96,2048]{1,0:T(8,128)(2,1)S(1)}, u32[]{:S(2)}, u32[]{:S(2)}) collective-permute-start(bf16[96,2048]{1,0:T(8,128)(2,1)S(1)} %get-tuple-element.79.refs_11_), channel_id=1, source_target_pairs={{0,16},{8,24},{16,0},{24,8},{1,17},{9,25},{17,1},{25,9},{2,18},{10... | collective-permute-start | bytes 1179656 | tf_op jit(solution)/shard_map/ppermute | solution.py:17
  255.3 25.5 %collective-permute-start.62 = (bf16[96,2048]{1,0:T(8,128)(2,1)S(1)}, bf16[96,2048]{1,0:T(8,128)(2,1)S(1)}, u32[]{:S(2)}, u32[]{:S(2)}) collective-permute-start(bf16[96,2048]{1,0:T(8,128)(2,1)S(1)} %get-tuple-element.77.refs_10_), channel_id=1, source_target_pairs={{0,8},{8,0},{16,24},{24,16},{1,9},{9,1},{17,25},{25,17},{2,10},{10... | collective-permute-start | bytes 1179656 | tf_op jit(solution)/shard_map/ppermute | solution.py:17
  262.6 18.3 %collective-permute-start.56 = (bf16[96,2048]{1,0:T(8,128)(2,1)S(1)}, bf16[96,2048]{1,0:T(8,128)(2,1)S(1)}, u32[]{:S(2)}, u32[]{:S(2)}) collective-permute-start(bf16[96,2048]{1,0:T(8,128)(2,1)S(1)} %get-tuple-element.82.refs_3_), channel_id=1, source_target_pairs={{0,4},{1,5},{2,6},{3,7},{4,0},{5,1},{6,2},{7,3},{8,12},{9,13},{10,... | collective-permute-start | bytes 1179656 | tf_op jit(solution)/shard_map/ppermute | solution.py:17
  264.6 11.6 %collective-permute-start.65 = (f32[1,8]{1,0:T(1,128)S(1)}, f32[1,8]{1,0:T(1,128)S(1)}, u32[]{:S(2)}, u32[]{:S(2)}) collective-permute-start(f32[1,8]{1,0:T(1,128)S(1)} %add.236), channel_id=1, source_target_pairs={{0,2},{1,3},{2,0},{3,1},{4,6},{5,7},{6,4},{7,5},{8,10},{9,11},{10,... | collective-permute-start | bytes 104 | tf_op jit(solution)/shard_map/ppermute | solution.py:17
  264.6 16.2 %collective-permute-start.60 = (bf16[96,2048]{1,0:T(8,128)(2,1)S(1)}, bf16[96,2048]{1,0:T(8,128)(2,1)S(1)}, u32[]{:S(2)}, u32[]{:S(2)}) collective-permute-start(bf16[96,2048]{1,0:T(8,128)(2,1)S(1)} %get-tuple-element.81.refs_3_), channel_id=1, source_target_pairs={{0,2},{1,3},{2,0},{3,1},{4,6},{5,7},{6,4},{7,5},{8,10},{9,11},{10,... | collective-permute-start | bytes 1179656 | tf_op jit(solution)/shard_map/ppermute | solution.py:17
  276.3 4.5 %collective-permute-start.66 = (f32[1,8]{1,0:T(1,128)S(1)}, f32[1,8]{1,0:T(1,128)S(1)}, u32[]{:S(2)}, u32[]{:S(2)}) collective-permute-start(f32[1,8]{1,0:T(1,128)S(1)} %add.237), channel_id=1, source_target_pairs={{0,4},{1,5},{2,6},{3,7},{4,0},{5,1},{6,2},{7,3},{8,12},{9,13},{10,... | collective-permute-start | bytes 104 | tf_op jit(solution)/shard_map/ppermute | solution.py:17
  281.4 13.1 %collective-permute-start.68 = (f32[4,32]{1,0:T(4,128)S(1)}, f32[4,32]{1,0:T(4,128)S(1)}, u32[]{:S(2)}, u32[]{:S(2)}) collective-permute-start(f32[4,32]{1,0:T(4,128)S(1)} %select_maximum_fusion), channel_id=1, source_target_pairs={{0,16},{8,24},{16,0},{24,8},{1,17},{9,25},{17,1},{25,9},{2,18},{10... | collective-permute-start | bytes 1544 | tf_op jit(solution)/shard_map/ppermute | solution.py:17
  281.5 13.1 %collective-permute-start.69 = (f32[4,32]{1,0:T(4,128)S(1)}, f32[4,32]{1,0:T(4,128)S(1)}, u32[]{:S(2)}, u32[]{:S(2)}) collective-permute-start(f32[4,32]{1,0:T(4,128)S(1)} %select_maximum_fusion), channel_id=1, source_target_pairs={{0,24},{8,16},{16,8},{24,0},{1,25},{9,17},{17,9},{25,1},{2,26},{10... | collective-permute-start | bytes 1544 | tf_op jit(solution)/shard_map/ppermute | solution.py:17
  283.5 11.1 %collective-permute-start.67 = (f32[4,32]{1,0:T(4,128)S(1)}, f32[4,32]{1,0:T(4,128)S(1)}, u32[]{:S(2)}, u32[]{:S(2)}) collective-permute-start(f32[4,32]{1,0:T(4,128)S(1)} %select_maximum_fusion), channel_id=1, source_target_pairs={{0,8},{8,0},{16,24},{24,16},{1,9},{9,1},{17,25},{25,17},{2,10},{10... | collective-permute-start | bytes 1544 | tf_op jit(solution)/shard_map/ppermute | solution.py:17
  (25 other events, 219.2 us)

commit v2 on v1

v2 whole, which is shorter than its diff:
```python
import functools
import jax
import jax.numpy as jnp
from jax import lax
from jax.experimental import pallas as pl
from jax.experimental.pallas import tpu as pltpu
from jax.sharding import PartitionSpec as P

epsilon = 1e-05
loss_scale = 1024.0
F32 = jnp.float32
BF16 = jnp.bfloat16
LANES = 128


def swap(x, axis, mask, size):
    return lax.ppermute(x, axis, [(i, i ^ mask) for i in range(size)])


def low(o):
    return o & -o


def high(o):
    return 1 << (o.bit_length() - 1)


def route(o, k):
    return low(o) if k & 1 else high(o)


def gather_order(sections, chips):
    single = [o for o in range(1, sections) if o.bit_count() == 1]
    several = sorted(
        (o for o in range(1, sections) if o.bit_count() > 1), key=lambda o: (o.bit_count(), o)
    )
    seq = []
    for k in range(chips + 1):
        if k < chips:
            seq += [("z", 0, c) for c in range(1, chips) if c ^ low(c) == k]
            seq += [("s", o, k) for o in single]
        if k:
            seq += [("s", o, k - 1) for o in several]
    return seq


def merge_kernel(masks, log, *refs):
    own, others, out = refs[0], refs[1:-1], refs[-1]
    n = own.shape[1]
    for b in range(n):
        row = pl.ds(b, 1)
        sources = [(own, row)] + [(r, pl.ds(b ^ m, 1)) for r, m in zip(others, masks)]
        tops = [r[0, at, :] for r, at in sources]
        top = functools.reduce(jnp.maximum, tops)
        total = functools.reduce(
            jnp.add, [r[1, at, :] * jnp.exp(t - top) for (r, at), t in zip(sources, tops)]
        )
        if log:
            out[row, :] = top + jnp.log(total)
        else:
            out[0, row, :] = top
            out[1, row, :] = total


def merge(own, others, masks, log=False):
    return pl.pallas_call(
        functools.partial(merge_kernel, masks, log),
        out_shape=jax.ShapeDtypeStruct(own.shape[1:] if log else own.shape, F32),
        compiler_params=pltpu.CompilerParams(vmem_limit_bytes=4 << 20),
        name="merge",
    )(own, *others)


def own_kernel(*refs):
    mine_ref, theirs_ref, weight_ref, out_ref = refs[1:]
    chips, rows, depth = mine_ref.shape
    states = jnp.concatenate(
        [mine_ref[...].reshape(chips * rows, depth), theirs_ref[...].reshape(chips * rows, depth)],
        axis=0,
    )
    out_ref[...] = jnp.dot(states, weight_ref[...], preferred_element_type=F32)


def own_pass(position, mine, theirs, weight):
    chips, rows, depth = mine.shape
    total_rows = 2 * chips * rows
    local = weight.shape[1]
    tile = min(512, local)
    piece = pl.BlockSpec(
        (chips, rows, depth), lambda i, pos: (0, 0, 0), pipeline_mode=pl.Buffered(1)
    )
    return pl.pallas_call(
        own_kernel,
        grid_spec=pltpu.PrefetchScalarGridSpec(
            num_scalar_prefetch=1,
            grid=(local // tile,),
            in_specs=[piece, piece, pl.BlockSpec((depth, tile), lambda i, pos: (pos[0], i))],
            out_specs=pl.BlockSpec((total_rows, tile), lambda i, pos: (0, i)),
        ),
        out_shape=jax.ShapeDtypeStruct((total_rows, local), F32),
        compiler_params=pltpu.CompilerParams(vmem_limit_bytes=24 << 20),
        cost_estimate=pl.CostEstimate(
            flops=2 * total_rows * depth * local,
            bytes_accessed=depth * (local + total_rows) * 2 + total_rows * local * 4,
            transcendentals=0,
        ),
        name="own_part",
    )(position, mine, theirs, weight)


def logits_kernel(offsets, chips, *refs):
    n = len(offsets)
    pieces, refs = refs[1 : 1 + 2 * n], refs[1 + 2 * n :]
    weights, refs = refs[:n], refs[n:]
    own_ref, out_ref, stat_ref, lhs, max_ref, sum_ref, even_ref, odd_ref, sem = refs
    rows = pieces[0].shape[1]
    step = pl.program_id(0)
    every = [(c, k) for c in range(2) for k in range(chips)]

    def incoming(g, c, k):
        return pltpu.make_async_copy(
            pieces[2 * g + c].at[k],
            lhs.at[g, pl.ds((c * chips + k) * rows, rows), :],
            sem.at[g, c, k],
        )

    columns = range(0, out_ref.shape[1], LANES)

    def absorb(held):
        for b in range(2 * chips):
            at = pl.ds(b * rows, rows)
            old = max_ref[at, :]
            new = functools.reduce(jnp.maximum, [held[at, pl.ds(c, LANES)] for c in columns], old)
            fresh = functools.reduce(
                jnp.add, [jnp.exp(held[at, pl.ds(c, LANES)] - new) for c in columns]
            )
            sum_ref[at, :] = sum_ref[at, :] * jnp.exp(old - new) + fresh
            max_ref[at, :] = new

    @pl.when(step == 0)
    def _():
        for g in range(n):
            for c, k in every:
                incoming(g, c, k).start()
        even_ref[...] = own_ref[...]
        for g in range(n):
            for c, k in every:
                incoming(g, c, k).wait()
            even_ref[...] += jnp.dot(lhs[g], weights[g][...], preferred_element_type=F32)
        out_ref[...] = even_ref[...]
        max_ref[...] = even_ref[:, :LANES]
        sum_ref[...] = jnp.zeros_like(sum_ref)

    for odd, (now, before) in enumerate(((even_ref, odd_ref), (odd_ref, even_ref))):

        @pl.when((step > 0) & (step % 2 == odd))
        def _():
            block = own_ref[...]
            for g in range(n):
                block += jnp.dot(lhs[g], weights[g][...], preferred_element_type=F32)
            absorb(before)
            out_ref[...] = block
            now[...] = block

    @pl.when(step == pl.num_programs(0) - 1)
    def _():
        absorb(out_ref)
        pad = jnp.ones((LANES - rows, LANES), F32)
        for b in range(2 * chips):
            at = pl.ds(b * rows, rows)
            top = jnp.max(max_ref[at, :], axis=1, keepdims=True)
            total = jnp.sum(sum_ref[at, :] * jnp.exp(max_ref[at, :] - top), axis=1, keepdims=True)
            for plane, value in enumerate((top, total)):
                tile = jnp.concatenate([jnp.broadcast_to(value, (rows, LANES)), pad], axis=0)
                stat_ref[plane, pl.ds(b, 1), :] = tile.T[:1, :]


def logits_pass(offsets, position, pieces, weight, own):
    n = len(offsets)
    chips, _, depth = pieces[0].shape
    total_rows, local = own.shape
    tile = min(256, local)
    stats = (2, 2 * chips, LANES)
    block = pl.BlockSpec((total_rows, tile), lambda i, pos: (0, i))

    def weight_spec(offset):
        return pl.BlockSpec((depth, tile), lambda i, pos: (pos[offset], i))

    return pl.pallas_call(
        functools.partial(logits_kernel, offsets, chips),
        grid_spec=pltpu.PrefetchScalarGridSpec(
            num_scalar_prefetch=1,
            grid=(local // tile,),
            in_specs=[pl.BlockSpec(memory_space=pl.ANY)] * (2 * n)
            + [weight_spec(o) for o in offsets]
            + [block],
            out_specs=[block, pl.BlockSpec(stats, lambda i, pos: (0, 0, 0))],
            scratch_shapes=[
                pltpu.VMEM((n, total_rows, depth), BF16),
                pltpu.VMEM((total_rows, LANES), F32),
                pltpu.VMEM((total_rows, LANES), F32),
                pltpu.VMEM((total_rows, tile), F32),
                pltpu.VMEM((total_rows, tile), F32),
                pltpu.SemaphoreType.DMA((n, 2, chips)),
            ],
        ),
        out_shape=[
            jax.ShapeDtypeStruct((total_rows, local), F32),
            jax.ShapeDtypeStruct(stats, F32),
        ],
        compiler_params=pltpu.CompilerParams(vmem_limit_bytes=29 << 20),
        cost_estimate=pl.CostEstimate(
            flops=2 * total_rows * n * depth * local,
            bytes_accessed=n * depth * (local + total_rows) * 2 + total_rows * local * 8,
            transcendentals=total_rows * local,
        ),
        name="logits",
    )(position, *pieces, *[weight] * n, own)


def delta_kernel(exits, scale, chips, logits_ref, norm_ref, *refs):
    teachers, (delta_ref, div_ref) = refs[:chips], refs[chips:]
    b = pl.program_id(0)

    @pl.when(b == 0)
    def _():
        div_ref[...] = jnp.zeros_like(div_ref)

    rows = logits_ref.shape[0]
    tokens = rows // exits
    for k in range(chips):

        @pl.when(b % chips == k)
        def _():
            line = jnp.broadcast_to(norm_ref[pl.ds(b, 1), :], (LANES, LANES))
            column = line.T[:rows, :1]
            teacher = teachers[k][b // chips]
            target = jnp.exp(teacher)
            for e in range(exits):
                part = pl.ds(e * tokens, tokens)
                shifted = logits_ref[part, :] - column[e * tokens : (e + 1) * tokens]
                delta_ref[part, :] = ((jnp.exp(shifted) - target) * scale).astype(BF16)
                gap = jnp.sum(target * (teacher - shifted), axis=0, keepdims=True)
                gap = jnp.sum(gap, axis=1, keepdims=True)
                div_ref[pl.ds(e, 1), :] += jnp.broadcast_to(gap, (1, LANES))


def delta_pass(logits, teachers, log_total, exits, scale):
    total_rows, local = logits.shape
    chips = len(teachers)
    tokens = teachers[0].shape[1]
    n_blocks = 2 * chips
    rows = exits * tokens
    pair = pl.BlockSpec(
        (2, tokens, local), lambda b: (0, 0, 0), pipeline_mode=pl.Buffered(1)
    )
    return pl.pallas_call(
        functools.partial(delta_kernel, exits, scale, chips),
        grid=(n_blocks,),
        in_specs=[
            pl.BlockSpec((rows, local), lambda b: (b, 0)),
            pl.BlockSpec((n_blocks, LANES), lambda b: (0, 0)),
        ]
        + [pair] * chips,
        out_specs=[
            pl.BlockSpec((rows, local), lambda b: (b, 0)),
            pl.BlockSpec((8, LANES), lambda b: (0, 0)),
        ],
        out_shape=[
            jax.ShapeDtypeStruct((total_rows, local), BF16),
            jax.ShapeDtypeStruct((8, LANES), F32),
        ],
        compiler_params=pltpu.CompilerParams(vmem_limit_bytes=9 << 20),
        cost_estimate=pl.CostEstimate(
            flops=total_rows * local * 8,
            bytes_accessed=total_rows * local * 6 + n_blocks * tokens * local * 4,
            transcendentals=total_rows * local,
        ),
        name="delta",
    )(logits, log_total, *teachers)


def state_grad_kernel(n_after, *refs):
    delta_ref, weight_ref = refs[1:3]
    keep_ref, send_ref = refs[3 + n_after :]
    chips, rows = keep_ref.shape[1:3]
    part = lax.dot_general(
        delta_ref[...], weight_ref[...], (((1,), (1,)), ((), ())), preferred_element_type=F32
    ).astype(BF16)
    for k in range(chips):
        keep_ref[0, k] = part[k * rows : (k + 1) * rows]
        send_ref[0, k] = part[(chips + k) * rows : (chips + k + 1) * rows]


def state_grad(places, delta, weight, chips, sections, after):
    n = places.shape[0]
    total_rows, local = delta.shape
    rows = total_rows // (2 * chips)
    depth = weight.shape[0] // sections
    tile = min(512, depth)
    steps = depth // tile
    spec = pl.BlockSpec((1, chips, rows, tile), lambda g, i, pos: (g, 0, 0, i))
    shape = jax.ShapeDtypeStruct((n, chips, rows, depth), BF16)
    return pl.pallas_call(
        functools.partial(state_grad_kernel, len(after)),
        grid_spec=pltpu.PrefetchScalarGridSpec(
            num_scalar_prefetch=1,
            grid=(n, steps),
            in_specs=[
                pl.BlockSpec(
                    (total_rows, local), lambda g, i, pos: (0, 0), pipeline_mode=pl.Buffered(1)
                ),
                pl.BlockSpec((tile, local), lambda g, i, pos: (pos[g] * steps + i, 0)),
            ]
            + [pl.BlockSpec(memory_space=pl.ANY)] * len(after),
            out_specs=[spec, spec],
        ),
        out_shape=[shape, shape],
        compiler_params=pltpu.CompilerParams(vmem_limit_bytes=17 << 20),
        cost_estimate=pl.CostEstimate(
            flops=2 * n * total_rows * depth * local,
            bytes_accessed=n * depth * (local + total_rows) * 2 + total_rows * local * 2,
            transcendentals=0,
        ),
        name="to_states",
    )(places, delta, weight, *after)


def head_grad_kernel(n, steps, *refs):
    delta_ref = refs[1 + 2 * n]
    step = pl.program_id(0)
    chips, rows, tile = refs[1].shape
    for g in range(n):
        mine_ref, theirs_ref = refs[1 + 2 * g : 3 + 2 * g]

        @pl.when((step >= g * steps) & (step < (g + 1) * steps))
        def _():
            states = jnp.concatenate(
                [
                    mine_ref[...].reshape(chips * rows, tile),
                    theirs_ref[...].reshape(chips * rows, tile),
                ],
                axis=0,
            )
            refs[-1][...] = lax.dot_general(
                states, delta_ref[...], (((0,), (0,)), ((), ())), preferred_element_type=F32
            ).astype(BF16)


def head_grad(places, states, delta, out, after, sections):
    n = len(states)
    chips, rows, depth = states[0][0].shape
    total_rows, local = delta.shape
    tile = min(512, depth)
    steps = depth // tile
    extra = list(after) + ([] if out is None else [out])

    def piece(g):
        return pl.BlockSpec(
            (chips, rows, tile), lambda i, pos: (0, 0, jnp.clip(i - g * steps, 0, steps - 1))
        )

    return pl.pallas_call(
        functools.partial(head_grad_kernel, n, steps),
        grid_spec=pltpu.PrefetchScalarGridSpec(
            num_scalar_prefetch=1,
            grid=(n * steps,),
            in_specs=[piece(g) for g in range(n) for _ in range(2)]
            + [
                pl.BlockSpec(
                    (total_rows, local), lambda i, pos: (0, 0), pipeline_mode=pl.Buffered(1)
                ),
            ]
            + [pl.BlockSpec(memory_space=pl.ANY)] * len(extra),
            out_specs=pl.BlockSpec(
                (tile, local), lambda i, pos: (pos[i // steps] * steps + i % steps, 0)
            ),
        ),
        out_shape=jax.ShapeDtypeStruct((sections * depth, local), BF16),
        input_output_aliases={} if out is None else {1 + 2 * n + len(extra): 0},
        compiler_params=pltpu.CompilerParams(vmem_limit_bytes=17 << 20),
        cost_estimate=pl.CostEstimate(
            flops=2 * n * total_rows * depth * local,
            bytes_accessed=n * depth * (local + total_rows) * 2 + total_rows * local * 2,
            transcendentals=0,
        ),
        name="to_head",
    )(places, *[block for pair in states for block in pair], delta, *extra)


def send_groups(sections, chips):
    groups = []
    half = chips // 2
    for count in range(sections.bit_length() - 1, 0, -1):
        offsets = [o for o in range(1, sections) if o.bit_count() == count]
        if count > 1:
            parts = [tuple(k for k in reversed(range(chips)) if k & 1 == odd) for odd in (1, 0)]
        else:
            parts = [(k,) for k in reversed(range(half, chips))]
            parts.append(tuple(reversed(range(half))))
        groups += [(o, ks) for ks in parts for o in offsets]
    return groups


def body(sections, vocabs, exit_hidden, norm_gain, head_weight, teacher):
    chips = vocabs // 2
    exits, tokens, depth = exit_hidden.shape
    rows = exits * tokens
    local = head_weight.shape[1]
    width = depth * sections
    all_tokens = tokens * vocabs
    section = lax.axis_index("section")
    vocab = lax.axis_index("vocab")
    position = jnp.stack([section ^ o for o in range(sections)]).astype(jnp.int32)

    def sec(x, mask):
        return swap(x, "section", mask, sections)

    def voc(x, mask):
        return swap(x, "vocab", mask, vocabs)

    def sec_sum(x):
        parts = [x]
        for o in range(1, sections):
            parts.append(sec(x, o))
        return functools.reduce(jnp.add, parts)

    order = sorted(range(sections), key=lambda o: (o.bit_count(), o))
    mine = [[None] * chips for _ in range(sections)]
    mine[0][0] = exit_hidden.reshape(rows, depth)
    for kind, o, k in gather_order(sections, chips):
        if kind == "z":
            mine[o][k] = voc(mine[0][k ^ low(k)], 2 * low(k))
        else:
            bit = route(o, k)
            mine[o][k] = sec(mine[o ^ bit][k], bit)

    hidden = exit_hidden.astype(F32)
    gains = norm_gain[:, None, :]
    squares = sec_sum(jnp.sum(hidden * hidden, axis=-1))
    inverse = lax.rsqrt(squares / width + epsilon)
    inverses = [inverse] + [voc(inverse, 2 * k) for k in range(1, chips)]
    inverse = inverse[..., None]
    normed, theirs, last = [None] * sections, [None] * sections, None
    for o in order:
        gain = (sec(norm_gain, o) if o else norm_gain)[:, None, :]
        raw = mine[o]
        if last is not None:
            *raw, _ = lax.optimization_barrier((*raw, last))
        blocks = [
            (raw[k].reshape(exits, tokens, depth).astype(F32) * inverses[k][..., None] * gain)
            .astype(BF16)
            .reshape(rows, depth)
            for k in range(chips)
        ]
        last = normed[o] = jnp.stack(blocks)
        theirs[o] = voc(normed[o], 1)

    def column_block(mask):
        return lax.dynamic_slice_in_dim(teacher, (vocab ^ mask) * local, local, axis=1)

    keep = [column_block(2 * k) for k in range(chips)]
    other = voc(jnp.stack([column_block(2 * k + 1) for k in range(chips)]), 1)
    teachers = [jnp.stack([keep[0], other[0]])]
    for k in range(1, chips):
        pair = jnp.stack([keep[k], other[k]])
        pair, _ = lax.optimization_barrier((pair, mine[0][-1]))
        teachers.append(voc(pair, 2 * k))

    own = own_pass(position, normed[0], theirs[0], head_weight)
    pieces = [block for o in order[1:] for block in (normed[o], theirs[o])]
    logits, stats = logits_pass(order[1:], position, pieces, head_weight, own)
    others = [sec(stats, o) for o in range(1, sections)]
    stats = merge(stats, others, [0] * len(others))
    others = [voc(stats, 2 * k) for k in range(1, chips)]
    stats = merge(stats, others, list(range(1, chips)))
    log_total = merge(stats, [voc(stats, 1)], [chips], log=True)

    delta, gaps = delta_pass(logits, teachers, log_total, exits, loss_scale / all_tokens)

    kept, got, moved = {}, {}, {}

    def places(offsets):
        return jnp.stack([section ^ o for o in offsets]).astype(jnp.int32)

    def total_of(o, k, token=None):
        blocks = [kept[o][k], got[o][k], *moved.get((o, k), ())]
        if token is not None:
            *blocks, _ = lax.optimization_barrier((*blocks, token))
        return functools.reduce(jnp.add, [block.astype(F32) for block in blocks])

    def send(o, ks):
        packed = {}
        for bit in sorted({route(o, k) for k in ks}):
            group = [k for k in ks if route(o, k) == bit]
            packed[bit] = jnp.stack([total_of(o, k).astype(BF16) for k in group])
            arrived = sec(packed[bit], bit)
            for i, k in enumerate(group):
                moved.setdefault((o ^ bit, k), []).append(arrived[i])
        return list(packed.values())

    groups = send_groups(sections, chips)
    backward = list(reversed(order))
    levels = [[o] for o in backward]
    after = []
    for index, level in enumerate(levels):
        kept_level, sent = state_grad(
            places(level), delta, head_weight, chips, sections, after
        )
        got_level = voc(sent, 1)
        for g, o in enumerate(level):
            kept[o], got[o] = kept_level[g], got_level[g]
        after = [kept_level]
        if index == 1:
            for group in groups:
                if group[0] == sections - 1:
                    after += send(*group)
    for group in groups:
        if group[0] != sections - 1:
            after += send(*group)

    sums = {}
    chain = []
    for k in range(chips - 1, 0, -1):
        total = sums.pop(k, 0.0) + total_of(0, k, chain[-1] if chain else None)
        packed = total.astype(BF16)
        chain.append(packed)
        arrived = voc(packed, 2 * low(k))
        sums[k ^ low(k)] = sums.get(k ^ low(k), 0.0) + arrived.astype(F32)
    own_sum = sums[0] + total_of(0, 0)

    calls = [[o] for o in range(sections)]
    share = -(-len(chain) // (len(calls) - 1))
    grad_head = None
    for index, offsets in enumerate(calls):
        if index:
            after = chain[(index - 1) * share : index * share]
        grad_head = head_grad(
            places(offsets), [(normed[o], theirs[o]) for o in offsets],
            delta, grad_head, after, sections,
        )

    gap = gaps[:, :1].reshape(1, 8)
    gates = [kept[0], *chain]
    for index in range(vocabs.bit_length() - 1):
        gap, _ = lax.optimization_barrier((gap, gates[min(index, len(gates) - 1)]))
        gap = gap + voc(gap, 1 << index)

    grad_normed = own_sum.reshape(exits, tokens, depth)
    weighted = gains * grad_normed
    inner = jnp.sum(weighted * hidden, axis=-1)
    gap_row = jnp.pad(gap[:, :exits], ((0, 0), (0, tokens - exits)))
    joined = sec_sum(jnp.concatenate([inner, gap_row], axis=0))
    divergence = joined[exits, :exits] / all_tokens
    inner = joined[:exits][..., None]
    grad_hidden = (inverse * weighted - hidden * inverse**3 * inner / width).astype(BF16)
    return divergence, grad_hidden, grad_head


def solution(mesh):
    sections, vocabs = mesh.shape["section"], mesh.shape["vocab"]
    return jax.shard_map(
        functools.partial(body, sections, vocabs),
        mesh=mesh,
        in_specs=(
            P(None, "vocab", "section"),
            P(None, "section"),
            P(None, ("section", "vocab")),
            P("vocab", "section"),
        ),
        out_specs=(P(), P(None, "vocab", "section"), P(None, ("section", "vocab"))),
        check_vma=False,
    )
```

time: 297 us -> 294 us (0.990)
  Pallas kernels: 132 us -> 121 us
  local copies, waits for them, and re-layouts: 12.3 us -> 5.13 us
  starting transfers between devices: 58 us -> 63.6 us
  other arithmetic: 9.36 us -> 14.4 us
  waiting for transfers between devices: 83.1 us -> 87.6 us
    pallas_call x12 -> x11, Pallas kernels: 132 us -> 121 us  [the longest x4 36.7 us: state_grad(): pl.pallas_call(functools.partial(state_grad_kernel, len(after)), grid_spe...]
    ppermute x70 -> x60, starting transfers between devices: 58 us -> 63.6 us  [swap(): return lax.ppermute(x, axis, [(i, i ^ mask) for i in range(size)])]
    unnamed x41 -> x26, local copies, waits for them, and re-layouts: 7.53 us -> 2.13 us
    convert_element_type x6 -> x10, other arithmetic: 3.17 us -> 8.24 us  [the longest x5 6.37 us: body(): blocks = [(raw[k].reshape(exits, tokens, depth).astype(F32) * inverses[k]...]
    ppermute x70 -> x60, waiting for transfers between devices: 83.1 us -> 87.6 us  [swap(): return lax.ppermute(x, axis, [(i, i ^ mask) for i in range(size)])]
  transfers between devices with their start and end apart: 70 -> 60, of which waited for: 22 -> 24; matrix products, arithmetic and copies ran while one was open for 4% -> 5% of each run, Pallas kernels for 40% -> 37%
where the time goes in v2:
time: 294 us; the launch traced here: 293 us
  Pallas kernels  121 us (41%)
  waiting for transfers between devices  87.6 us (30%)
  starting transfers between devices  63.6 us (22%)
  other arithmetic  14.4 us (5%)
  local copies, waits for them, and re-layouts  5.13 us (2%)
    ppermute x60, waiting for transfers between devices, swap(): return lax.ppermute(x, axis, [(i, i ^ mask) for i in range(size)])  87.6 us
    ppermute x60, starting transfers between devices, swap(): return lax.ppermute(x, axis, [(i, i ^ mask) for i in range(size)])  63.6 us
    pallas_call x4, Pallas kernels, state_grad(): pl.pallas_call(functools.partial(state_grad_kernel, len(after)), grid_spe...  36.7 us
    pallas_call x4, Pallas kernels, head_grad(): pl.pallas_call(functools.partial(head_grad_kernel, n, steps), grid_spec=p...  36.3 us
    pallas_call x1, Pallas kernels, logits_pass(): pl.pallas_call(functools.partial(logits_kernel, offsets, chips), grid_spe...  34 us
    pallas_call x1, Pallas kernels, own_pass(): pl.pallas_call(own_kernel, grid_spec=pltpu.PrefetchScalarGridSpec(num_sca...  9.88 us
    convert_element_type x5, other arithmetic, body(): blocks = [(raw[k].reshape(exits, tokens, depth).astype(F32) * inverses[k]...  6.37 us
  transfers between devices with their start and end apart: 60, of which 24 were waited for; matrix products, arithmetic and copies ran while one was open for 5% of the time, Pallas kernels for 37%

profile of v2, /device:TPU:0, one launch (start us, length us, event | category | flops | bytes accessed | tf_op | source)
XLA Modules:
  0.0 293.3 jit_solution(13311331367544378991)
XLA Ops:
  0.6 4.1 %collective-permute-start.3 = (bf16[96,2048]{1,0:T(8,128)(2,1)}, bf16[96,2048]{1,0:T(8,128)(2,1)}, u32[]{:S(2)}, u32[]{:S(2)}) collective-permute-start(bf16[96,2048]{1,0:T(8,128)(2,1)} %bitcast.160), channel_id=1, source_target_pairs={{0,4},{1,5},{2,6},{3,7},{4,0},{5,1},{6,2},{7,3},{8,12},{9,13},{10,... | collective-permute-start | bytes 1179656 | tf_op jit(solution)/shard_map/ppermute | solution.py:17
  4.8 1.5 collective-permute-start.15
  7.5 1.5 collective-permute-start.9
  9.0 1.5 collective-permute-start.8
  12.1 1.5 collective-permute-start.13
  13.6 2.0 collective-permute-done.8
  15.6 1.5 collective-permute-start.19
  17.8 1.4 collective-permute-start.12
  19.1 4.0 %collective-permute-done.12 = f32[3,32]{1,0:T(4,128)S(1)} collective-permute-done((f32[3,32]{1,0:T(4,128)S(1)}, f32[3,32]{1,0:T(4,128)S(1)}, u32[]{:S(2)}, u32[]{:S(2)}) %collective-permute-start.12) | collective-permute-done | bytes 416 | tf_op jit(solution)/shard_map/ppermute | solution.py:17
  23.1 2.1 collective-permute-start.11
  25.2 2.4 collective-permute-done.11
  27.9 3.5 %collective-permute-done.10 = f32[3,32]{1,0:T(4,128)} collective-permute-done((f32[3,32]{1,0:T(4,128)S(1)}, f32[3,32]{1,0:T(4,128)}, u32[]{:S(2)}, u32[]{:S(2)}) %collective-permute-start.10) | collective-permute-done | bytes 416 | tf_op jit(solution)/shard_map/ppermute | solution.py:17
  31.6 1.5 collective-permute-start
  33.1 1.5 collective-permute-start.17
  36.8 1.6 dynamic-slice_bitcast_fusion
  38.7 5.0 %collective-permute-done.1 = bf16[96,2048]{1,0:T(8,128)(2,1)} collective-permute-done((bf16[96,2048]{1,0:T(8,128)(2,1)}, bf16[96,2048]{1,0:T(8,128)(2,1)}, u32[]{:S(2)}, u32[]{:S(2)}) %collective-permute-start.1) | collective-permute-done | bytes 393248 | tf_op jit(solution)/shard_map/ppermute | solution.py:17
  44.3 1.5 collective-permute-start.2
  45.8 1.4 collective-permute-start.21
  48.0 1.5 collective-permute-start.18
  49.5 2.8 collective-permute-done.4
  52.3 1.5 collective-permute-start.6
  55.8 1.6 fusion.8
  57.4 3.4 %collective-permute-done.2 = bf16[96,2048]{1,0:T(8,128)(2,1)} collective-permute-done((bf16[96,2048]{1,0:T(8,128)(2,1)}, bf16[96,2048]{1,0:T(8,128)(2,1)}, u32[]{:S(2)}, u32[]{:S(2)}) %collective-permute-start.2) | collective-permute-done | bytes 393248 | tf_op jit(solution)/shard_map/ppermute | solution.py:17
  60.7 4.9 %collective-permute-done.6 = bf16[96,2048]{1,0:T(8,128)(2,1)} collective-permute-done((bf16[96,2048]{1,0:T(8,128)(2,1)}, bf16[96,2048]{1,0:T(8,128)(2,1)}, u32[]{:S(2)}, u32[]{:S(2)}) %collective-permute-start.6) | collective-permute-done | bytes 393248 | tf_op jit(solution)/shard_map/ppermute | solution.py:17
  65.6 1.5 collective-permute-start.23
  67.9 1.8 fusion.11
  69.8 1.6 collective-permute-start.22
  72.9 1.7 fusion.15
  75.2 1.5 collective-permute-start.25
  76.8 5.2 %collective-permute-done.22 = bf16[96,2048]{1,0:T(8,128)(2,1)S(1)} collective-permute-done((bf16[96,2048]{1,0:T(8,128)(2,1)}, bf16[96,2048]{1,0:T(8,128)(2,1)S(1)}, u32[]{:S(2)}, u32[]{:S(2)}) %collective-permute-start.22) | collective-permute-done | bytes 393248 | tf_op jit(solution)/shard_map/ppermute | solution.py:17
  82.0 8.2 %collective-permute-done.24 = bf16[96,2048]{1,0:T(8,128)(2,1)S(1)} collective-permute-done((bf16[96,2048]{1,0:T(8,128)(2,1)}, bf16[96,2048]{1,0:T(8,128)(2,1)S(1)}, u32[]{:S(2)}, u32[]{:S(2)}) %collective-permute-start.24) | collective-permute-done | bytes 393248 | tf_op jit(solution)/shard_map/ppermute | solution.py:17
  91.7 2.0 collective-permute-start.37
  93.7 1.7 collective-permute-start.36
  95.4 9.9 %own_part.1.refs_10_ = f32[768,2048]{1,0:T(8,128)S(1)} custom-call(s32[4]{0:T(128)S(1)} %pad_add_fusion.refs_0_, bf16[4,96,2048]{2,1,0:T(8,128)(2,1)S(1)} %pad_maximum_fusion.refs_1_, bf16[4,96,2048]{2,1,0:T(8,128)(2,1)S(1)} %collective-permute-done.27.refs_2_, bf16[8192,2048]{1,0:T(8,128)(2,1)} %refs_2_.7), custom_call_target="tpu_custom_call" | custom-call | flops 6442450944 | bytes 17825792 | tf_op jit(solution)/shard_map/own_part/pallas_call | solution.py:92
  106.1 34.0 %logits.1 = (f32[768,2048]{1,0:T(8,128)S(1)}, f32[2,8,128]{2,1,0:T(8,128)S(1)}) custom-call(s32[4]{0:T(128)S(1)} %pad_add_fusion.refs_0_, bf16[4,96,2048]{2,1,0:T(8,128)(2,1)S(1)} %pad_maximum_fusion.1.refs_1_, bf16[4,96,2048]{2,1,0:T(8,128)(2,1)S(1)} %collective-permute-done.14.refs_2_, bf16[4,96,2048]{2,1,0:T(8,128)(2,1)S(1)} %pad_maximum_fusion.2.refs_3_.refs_1_, ...), custom_call_target="tpu_custom_call" | custom-call | flops 19327352832 | bytes 47185920 | tf_op jit(solution)/shard_map/logits/pallas_call | solution.py:189
  140.1 2.3 collective-permute-start.30
  143.2 1.6 collective-permute-done.30.refs_3_
  144.8 1.5 collective-permute-start.28
  146.3 2.2 collective-permute-done.28.refs_1_
  148.5 3.1 %collective-permute-start.33 = (f32[2,8,128]{2,1,0:T(8,128)S(1)}, f32[2,8,128]{2,1,0:T(8,128)S(1)}, u32[]{:S(2)}, u32[]{:S(2)}) collective-permute-start(f32[2,8,128]{2,1,0:T(8,128)S(1)} %merge.3.refs_0_), channel_id=1, source_target_pairs={{0,6},{1,7},{2,4},{3,5},{4,2},{5,3},{6,0},{7,1},{8,14},{9,15},{10,... | collective-permute-start | bytes 24584 | tf_op jit(solution)/shard_map/ppermute | solution.py:17
  151.5 2.5 collective-permute-done.33.refs_3_
  154.0 2.1 collective-permute-done.32.refs_2_
  156.1 1.6 collective-permute-done.31.refs_1_
  159.0 4.4 %delta.1 = (bf16[768,2048]{1,0:T(8,128)(2,1)S(1)}, f32[8,128]{1,0:T(8,128)S(1)}) custom-call(f32[768,2048]{1,0:T(8,128)S(1)} %get-tuple-element.52.logits_ref, f32[8,128]{1,0:T(8,128)S(1)} %merge.5.norm_ref, f32[2,32,2048]{2,1,0:T(8,128)S(1)} %pad_maximum_fusion.9.refs_0_, f32[2,32,2048]{2,1,0:T(8,128)S(1)} %collective-permute-done.36.refs_1_, ...), custom_call_target="tpu_custom_call" | custom-call | flops 12582912 | bytes 11534336 | tf_op jit(solution)/shard_map/delta/pallas_call | solution.py:257
  163.4 9.3 %to_states.4 = (bf16[1,4,96,2048]{3,2,1,0:T(8,128)(2,1)S(1)}, bf16[1,4,96,2048]{3,2,1,0:T(8,128)(2,1)S(1)}) custom-call(s32[1]{0:T(128)} %bitcast.3.refs_0_, bf16[768,2048]{1,0:T(8,128)(2,1)S(1)} %get-tuple-element.57.refs_1_.refs_3_, bf16[8192,2048]{1,0:T(8,128)(2,1)} %refs_2_.7), custom_call_target="tpu_custom_call" | custom-call | flops 6442450944 | bytes 14680064 | tf_op jit(solution)/shard_map/to_states/pallas_call | solution.py:304
  173.5 9.1 %to_states.5 = (bf16[1,4,96,2048]{3,2,1,0:T(8,128)(2,1)S(1)}, bf16[1,4,96,2048]{3,2,1,0:T(8,128)(2,1)S(1)}) custom-call(s32[1]{0:T(128)} %bitcast.2.refs_0_, bf16[768,2048]{1,0:T(8,128)(2,1)S(1)} %get-tuple-element.57.refs_1_.refs_3_, bf16[8192,2048]{1,0:T(8,128)(2,1)} %refs_2_.7, bf16[1,4,96,2048]{3,2,1,0:T(8,128)(2,1)S(1)} %get-tuple-element.58.refs_3_), custom_call_target="tpu_custom_call" | custom-call | flops 6442450944 | bytes 14680064 | tf_op jit(solution)/shard_map/to_states/pallas_call | solution.py:304
  183.5 1.6 collective-permute-start.44
  185.2 1.3 collective-permute-start.47
  186.5 9.1 %to_states.6 = (bf16[1,4,96,2048]{3,2,1,0:T(8,128)(2,1)S(1)}, bf16[1,4,96,2048]{3,2,1,0:T(8,128)(2,1)S(1)}) custom-call(s32[1]{0:T(128)} %bitcast.1.refs_0_, bf16[768,2048]{1,0:T(8,128)(2,1)S(1)} %get-tuple-element.57.refs_1_.refs_3_, bf16[8192,2048]{1,0:T(8,128)(2,1)} %refs_2_.7, bf16[1,4,96,2048]{3,2,1,0:T(8,128)(2,1)S(1)} %get-tuple-element.59.refs_3_, ...), custom_call_target="tpu_custom_call" | custom-call | flops 6442450944 | bytes 14680064 | tf_op jit(solution)/shard_map/to_states/pallas_call | solution.py:304
  195.7 9.1 %to_states.7 = (bf16[1,4,96,2048]{3,2,1,0:T(8,128)(2,1)S(1)}, bf16[1,4,96,2048]{3,2,1,0:T(8,128)(2,1)S(1)}) custom-call(s32[1]{0:T(128)} %bitcast.refs_0_, bf16[768,2048]{1,0:T(8,128)(2,1)S(1)} %get-tuple-element.57.refs_1_.refs_3_, bf16[8192,2048]{1,0:T(8,128)(2,1)} %refs_2_.7, bf16[1,4,96,2048]{3,2,1,0:T(8,128)(2,1)S(1)} %get-tuple-element.61.refs_3_), custom_call_target="tpu_custom_call" | custom-call | flops 6442450944 | bytes 14680064 | tf_op jit(solution)/shard_map/to_states/pallas_call | solution.py:304
  207.0 1.3 collective-permute-start.45
  210.5 1.5 collective-permute-start.42
  212.2 9.1 %to_head.4.refs_5_ = bf16[8192,2048]{1,0:T(8,128)(2,1)} custom-call(s32[1]{0:T(128)} %bitcast.refs_0_, bf16[4,96,2048]{2,1,0:T(8,128)(2,1)S(1)} %pad_maximum_fusion.refs_1_, bf16[4,96,2048]{2,1,0:T(8,128)(2,1)S(1)} %collective-permute-done.27.refs_2_, bf16[768,2048]{1,0:T(8,128)(2,1)S(1)} %get-tuple-element.57.refs_1_.refs_3_, ...), custom_call_target="tpu_custom_call" | custom-call | flops 6442450944 | bytes 14680064 | tf_op jit(solution)/shard_map/to_head/pallas_call | solution.py:363
  221.3 20.9 %collective-permute-done.52 = bf16[2,96,2048]{2,1,0:T(8,128)(2,1)S(1)} collective-permute-done((bf16[2,96,2048]{2,1,0:T(8,128)(2,1)S(1)}, bf16[2,96,2048]{2,1,0:T(8,128)(2,1)S(1)}, u32[]{:S(2)}, u32[]{:S(2)}) %collective-permute-start.52) | collective-permute-done | bytes 786464 | tf_op jit(solution)/shard_map/ppermute | solution.py:17
  243.1 2.0 collective-permute-start.55
  245.1 9.0 %to_head.5.refs_5_ = bf16[8192,2048]{1,0:T(8,128)(2,1)} custom-call(s32[1]{0:T(128)} %bitcast.1.refs_0_, bf16[4,96,2048]{2,1,0:T(8,128)(2,1)S(1)} %pad_maximum_fusion.1.refs_1_, bf16[4,96,2048]{2,1,0:T(8,128)(2,1)S(1)} %collective-permute-done.14.refs_2_, bf16[768,2048]{1,0:T(8,128)(2,1)S(1)} %get-tuple-element.57.refs_1_.refs_3_, ...), custom_call_target="tpu_custom_call", output_to_operand_aliasing={{}: (5, {})} | custom-call | flops 6442450944 | bytes 14680064 | tf_op jit(solution)/shard_map/to_head/pallas_call | solution.py:363
  254.5 1.7 collective-permute-start.50
  256.2 1.3 collective-permute-start.56
  257.5 3.3 %collective-permute-done.51 = bf16[2,96,2048]{2,1,0:T(8,128)(2,1)S(1)} collective-permute-done((bf16[2,96,2048]{2,1,0:T(8,128)(2,1)S(1)}, bf16[2,96,2048]{2,1,0:T(8,128)(2,1)S(1)}, u32[]{:S(2)}, u32[]{:S(2)}) %collective-permute-start.51) | collective-permute-done | bytes 786464 | tf_op jit(solution)/shard_map/ppermute | solution.py:17
  261.1 9.1 %to_head.6.refs_5_ = bf16[8192,2048]{1,0:T(8,128)(2,1)} custom-call(s32[1]{0:T(128)} %bitcast.2.refs_0_, bf16[4,96,2048]{2,1,0:T(8,128)(2,1)S(1)} %pad_maximum_fusion.2.refs_3_.refs_1_, bf16[4,96,2048]{2,1,0:T(8,128)(2,1)S(1)} %collective-permute-done.20.refs_4_.refs_2_, ...), custom_call_target="tpu_custom_call", output_to_operand_aliasing={{}: (5, {})} | custom-call | flops 6442450944 | bytes 14680064 | tf_op jit(solution)/shard_map/to_head/pallas_call | solution.py:363
  270.2 3.2 %collective-permute-done.56 = f32[1,8]{1,0:T(1,128)S(1)} collective-permute-done((f32[1,8]{1,0:T(1,128)S(1)}, f32[1,8]{1,0:T(1,128)S(1)}, u32[]{:S(2)}, u32[]{:S(2)}) %collective-permute-start.56) | collective-permute-done | bytes 64 | tf_op jit(solution)/shard_map/ppermute | solution.py:17
  273.4 4.9 %collective-permute-done.53 = bf16[96,2048]{1,0:T(8,128)(2,1)S(1)} collective-permute-done((bf16[96,2048]{1,0:T(8,128)(2,1)S(1)}, bf16[96,2048]{1,0:T(8,128)(2,1)S(1)}, u32[]{:S(2)}, u32[]{:S(2)}) %collective-permute-start.53) | collective-permute-done | bytes 393248 | tf_op jit(solution)/shard_map/ppermute | solution.py:17
  281.1 1.5 collective-permute-start.57
  282.5 9.0 %to_head.7 = bf16[8192,2048]{1,0:T(8,128)(2,1)} custom-call(s32[1]{0:T(128)} %bitcast.3.refs_0_, bf16[4,96,2048]{2,1,0:T(8,128)(2,1)S(1)} %pad_maximum_fusion.3.refs_5_.refs_1_, bf16[4,96,2048]{2,1,0:T(8,128)(2,1)S(1)} %collective-permute-done.26.refs_6_.refs_2_, ...), custom_call_target="tpu_custom_call", output_to_operand_aliasing={{}: (5, {})} | custom-call | flops 6442450944 | bytes 14680064 | tf_op jit(solution)/shard_map/to_head/pallas_call | solution.py:363
  (144 shorter events, 29.2 us)
Async XLA Ops:
  0.6 32.5 %collective-permute-start.3 = (bf16[96,2048]{1,0:T(8,128)(2,1)}, bf16[96,2048]{1,0:T(8,128)(2,1)}, u32[]{:S(2)}, u32[]{:S(2)}) collective-permute-start(bf16[96,2048]{1,0:T(8,128)(2,1)} %bitcast.160), channel_id=1, source_target_pairs={{0,4},{1,5},{2,6},{3,7},{4,0},{5,1},{6,2},{7,3},{8,12},{9,13},{10,... | collective-permute-start | bytes 1179656 | tf_op jit(solution)/shard_map/ppermute | solution.py:17
  4.8 30.8 %collective-permute-start.15 = (bf16[96,2048]{1,0:T(8,128)(2,1)}, bf16[96,2048]{1,0:T(8,128)(2,1)S(1)}, u32[]{:S(2)}, u32[]{:S(2)}) collective-permute-start(bf16[96,2048]{1,0:T(8,128)(2,1)} %bitcast.161), channel_id=1, source_target_pairs={{0,16},{8,24},{16,0},{24,8},{1,17},{9,25},{17,1},{25,9},{2,18},{10... | collective-permute-start | bytes 1179656 | tf_op jit(solution)/shard_map/ppermute | solution.py:17
  7.5 4.6 %collective-permute-start.9 = (f32[3,32]{1,0:T(4,128)S(1)}, f32[3,32]{1,0:T(4,128)S(1)}, u32[]{:S(2)}, u32[]{:S(2)}) collective-permute-start(f32[3,32]{1,0:T(4,128)S(1)} %fusion), channel_id=1, source_target_pairs={{0,24},{8,16},{16,8},{24,0},{1,25},{9,17},{17,9},{25,1},{2,26},{10... | collective-permute-start | bytes 1160 | tf_op jit(solution)/shard_map/ppermute | solution.py:17
  9.0 6.7 %collective-permute-start.8 = (f32[3,32]{1,0:T(4,128)S(1)}, f32[3,32]{1,0:T(4,128)S(1)}, u32[]{:S(2)}, u32[]{:S(2)}) collective-permute-start(f32[3,32]{1,0:T(4,128)S(1)} %fusion), channel_id=1, source_target_pairs={{0,16},{8,24},{16,0},{24,8},{1,17},{9,25},{17,1},{25,9},{2,18},{10... | collective-permute-start | bytes 1160 | tf_op jit(solution)/shard_map/ppermute | solution.py:17
  10.5 6.7 %collective-permute-start.7 = (f32[3,32]{1,0:T(4,128)S(1)}, f32[3,32]{1,0:T(4,128)S(1)}, u32[]{:S(2)}, u32[]{:S(2)}) collective-permute-start(f32[3,32]{1,0:T(4,128)S(1)} %fusion), channel_id=1, source_target_pairs={{0,8},{8,0},{16,24},{24,16},{1,9},{9,1},{17,25},{25,17},{2,10},{10... | collective-permute-start | bytes 1160 | tf_op jit(solution)/shard_map/ppermute | solution.py:17
  12.1 19.5 %collective-permute-start.13 = (f32[3,2048]{1,0:T(4,128)}, f32[3,2048]{1,0:T(4,128)S(1)}, u32[]{:S(2)}, u32[]{:S(2)}) collective-permute-start(f32[3,2048]{1,0:T(4,128)} %param.5), channel_id=1, source_target_pairs={{0,8},{8,0},{16,24},{24,16},{1,9},{9,1},{17,25},{25,17},{2,10},{10... | collective-permute-start | bytes 73736 | tf_op jit(solution)/shard_map/ppermute | solution.py:17
  15.6 19.0 %collective-permute-start.19 = (f32[3,2048]{1,0:T(4,128)}, f32[3,2048]{1,0:T(4,128)S(1)}, u32[]{:S(2)}, u32[]{:S(2)}) collective-permute-start(f32[3,2048]{1,0:T(4,128)} %param.5), channel_id=1, source_target_pairs={{0,16},{8,24},{16,0},{24,8},{1,17},{9,25},{17,1},{25,9},{2,18},{10... | collective-permute-start | bytes 73736 | tf_op jit(solution)/shard_map/ppermute | solution.py:17
  17.8 37.0 %copy-start.10 = (f32[3,32]{1,0:T(4,128)}, f32[3,32]{1,0:T(4,128)S(1)}, u32[]{:S(2)}) copy-start(f32[3,32]{1,0:T(4,128)S(1)} %get-tuple-element.78) | copy-start | bytes 1156
  17.8 5.4 %collective-permute-start.12 = (f32[3,32]{1,0:T(4,128)S(1)}, f32[3,32]{1,0:T(4,128)S(1)}, u32[]{:S(2)}, u32[]{:S(2)}) collective-permute-start(f32[3,32]{1,0:T(4,128)S(1)} %get-tuple-element.78), channel_id=1, source_target_pairs={{0,6},{1,7},{2,4},{3,5},{4,2},{5,3},{6,0},{7,1},{8,14},{9,15},{10,... | collective-permute-start | bytes 1160 | tf_op jit(solution)/shard_map/ppermute | solution.py:17
  23.1 4.5 %collective-permute-start.11 = (f32[3,32]{1,0:T(4,128)S(1)}, f32[3,32]{1,0:T(4,128)S(1)}, u32[]{:S(2)}, u32[]{:S(2)}) collective-permute-start(f32[3,32]{1,0:T(4,128)S(1)} %get-tuple-element.78), channel_id=1, source_target_pairs={{0,4},{1,5},{2,6},{3,7},{4,0},{5,1},{6,2},{7,3},{8,12},{9,13},{10,... | collective-permute-start | bytes 1160 | tf_op jit(solution)/shard_map/ppermute | solution.py:17
  27.6 3.7 %collective-permute-start.10 = (f32[3,32]{1,0:T(4,128)S(1)}, f32[3,32]{1,0:T(4,128)}, u32[]{:S(2)}, u32[]{:S(2)}) collective-permute-start(f32[3,32]{1,0:T(4,128)S(1)} %get-tuple-element.78), channel_id=1, source_target_pairs={{0,2},{1,3},{2,0},{3,1},{4,6},{5,7},{6,4},{7,5},{8,10},{9,11},{10,... | collective-permute-start | bytes 1160 | tf_op jit(solution)/shard_map/ppermute | solution.py:17
  31.3 12.3 %collective-permute-start.1 = (bf16[96,2048]{1,0:T(8,128)(2,1)}, bf16[96,2048]{1,0:T(8,128)(2,1)}, u32[]{:S(2)}, u32[]{:S(2)}) collective-permute-start(bf16[96,2048]{1,0:T(8,128)(2,1)} %bitcast.162), channel_id=1, source_target_pairs={{0,2},{1,3},{2,0},{3,1},{4,6},{5,7},{6,4},{7,5},{8,10},{9,11},{10,... | collective-permute-start | bytes 1179656 | tf_op jit(solution)/shard_map/ppermute | solution.py:17
  31.6 12.7 %collective-permute-start = (bf16[96,2048]{1,0:T(8,128)(2,1)}, bf16[96,2048]{1,0:T(8,128)(2,1)}, u32[]{:S(2)}, u32[]{:S(2)}) collective-permute-start(bf16[96,2048]{1,0:T(8,128)(2,1)} %bitcast.163), channel_id=1, source_target_pairs={{0,8},{8,0},{16,24},{24,16},{1,9},{9,1},{17,25},{25,17},{2,10},{10... | collective-permute-start | bytes 1179656 | tf_op jit(solution)/shard_map/ppermute | solution.py:17
  33.1 12.7 %collective-permute-start.17 = (bf16[96,2048]{1,0:T(8,128)(2,1)}, bf16[96,2048]{1,0:T(8,128)(2,1)}, u32[]{:S(2)}, u32[]{:S(2)}) collective-permute-start(bf16[96,2048]{1,0:T(8,128)(2,1)} %collective-permute-done.3), channel_id=1, source_target_pairs={{0,16},{8,24},{16,0},{24,8},{1,17},{9,25},{17,1},{25,9},{2,18},{10... | collective-permute-start | bytes 1179656 | tf_op jit(solution)/shard_map/ppermute | solution.py:17
  34.6 13.4 %collective-permute-start.5 = (bf16[96,2048]{1,0:T(8,128)(2,1)}, bf16[96,2048]{1,0:T(8,128)(2,1)}, u32[]{:S(2)}, u32[]{:S(2)}) collective-permute-start(bf16[96,2048]{1,0:T(8,128)(2,1)} %collective-permute-done.3), channel_id=1, source_target_pairs={{0,2},{1,3},{2,0},{3,1},{4,6},{5,7},{6,4},{7,5},{8,10},{9,11},{10,... | collective-permute-start | bytes 1179656 | tf_op jit(solution)/shard_map/ppermute | solution.py:17
  36.3 16.0 %collective-permute-start.4 = (bf16[96,2048]{1,0:T(8,128)(2,1)}, bf16[96,2048]{1,0:T(8,128)(2,1)}, u32[]{:S(2)}, u32[]{:S(2)}) collective-permute-start(bf16[96,2048]{1,0:T(8,128)(2,1)} %collective-permute-done.3), channel_id=1, source_target_pairs={{0,8},{8,0},{16,24},{24,16},{1,9},{9,1},{17,25},{25,17},{2,10},{10... | collective-permute-start | bytes 1179656 | tf_op jit(solution)/shard_map/ppermute | solution.py:17
  38.5 15.3 %copy-start = (bf16[3,32,2048]{2,1,0:T(8,128)(2,1)S(1)}, bf16[3,32,2048]{2,1,0:T(8,128)(2,1)}, u32[]{:S(2)}) copy-start(bf16[3,32,2048]{2,1,0:T(8,128)(2,1)} %param.4) | copy-start | bytes 1179652
  43.6 26.0 %collective-permute-start.16 = (bf16[96,2048]{1,0:T(8,128)(2,1)}, bf16[96,2048]{1,0:T(8,128)(2,1)}, u32[]{:S(2)}, u32[]{:S(2)}) collective-permute-start(bf16[96,2048]{1,0:T(8,128)(2,1)} %collective-permute-done.1), channel_id=1, source_target_pairs={{0,16},{8,24},{16,0},{24,8},{1,17},{9,25},{17,1},{25,9},{2,18},{10... | collective-permute-start | bytes 1179656 | tf_op jit(solution)/shard_map/ppermute | solution.py:17
  44.3 16.4 %collective-permute-start.2 = (bf16[96,2048]{1,0:T(8,128)(2,1)}, bf16[96,2048]{1,0:T(8,128)(2,1)}, u32[]{:S(2)}, u32[]{:S(2)}) collective-permute-start(bf16[96,2048]{1,0:T(8,128)(2,1)} %collective-permute-done.1), channel_id=1, source_target_pairs={{0,8},{8,0},{16,24},{24,16},{1,9},{9,1},{17,25},{25,17},{2,10},{10... | collective-permute-start | bytes 1179656 | tf_op jit(solution)/shard_map/ppermute | solution.py:17
  45.8 24.0 %collective-permute-start.21 = (bf16[96,2048]{1,0:T(8,128)(2,1)}, bf16[96,2048]{1,0:T(8,128)(2,1)S(1)}, u32[]{:S(2)}, u32[]{:S(2)}) collective-permute-start(bf16[96,2048]{1,0:T(8,128)(2,1)} %collective-permute-done), channel_id=1, source_target_pairs={{0,16},{8,24},{16,0},{24,8},{1,17},{9,25},{17,1},{25,9},{2,18},{10... | collective-permute-start | bytes 1179656 | tf_op jit(solution)/shard_map/ppermute | solution.py:17
  48.0 23.4 %collective-permute-start.18 = (bf16[96,2048]{1,0:T(8,128)(2,1)}, bf16[96,2048]{1,0:T(8,128)(2,1)}, u32[]{:S(2)}, u32[]{:S(2)}) collective-permute-start(bf16[96,2048]{1,0:T(8,128)(2,1)} %collective-permute-done.5), channel_id=1, source_target_pairs={{0,16},{8,24},{16,0},{24,8},{1,17},{9,25},{17,1},{25,9},{2,18},{10... | collective-permute-start | bytes 1179656 | tf_op jit(solution)/shard_map/ppermute | solution.py:17
  52.3 13.3 %collective-permute-start.6 = (bf16[96,2048]{1,0:T(8,128)(2,1)}, bf16[96,2048]{1,0:T(8,128)(2,1)}, u32[]{:S(2)}, u32[]{:S(2)}) collective-permute-start(bf16[96,2048]{1,0:T(8,128)(2,1)} %collective-permute-done.5), channel_id=1, source_target_pairs={{0,8},{8,0},{16,24},{24,16},{1,9},{9,1},{17,25},{25,17},{2,10},{10... | collective-permute-start | bytes 1179656 | tf_op jit(solution)/shard_map/ppermute | solution.py:17
  60.7 30.8 %collective-permute-start.35 = (f32[4,32,2048]{2,1,0:T(8,128)S(1)}, f32[4,32,2048]{2,1,0:T(8,128)S(1)}, u32[]{:S(2)}, u32[]{:S(2)}) collective-permute-start(f32[4,32,2048]{2,1,0:T(8,128)S(1)} %pad_maximum_fusion.4), channel_id=1, source_target_pairs={{0,1},{1,0},{2,3},{3,2},{4,5},{5,4},{6,7},{7,6},{8,9},{9,8},{10,11... | collective-permute-start | bytes 3145736 | tf_op jit(solution)/shard_map/ppermute | solution.py:17
  65.6 9.5 %collective-permute-start.23 = (bf16[96,2048]{1,0:T(8,128)(2,1)}, bf16[96,2048]{1,0:T(8,128)(2,1)S(1)}, u32[]{:S(2)}, u32[]{:S(2)}) collective-permute-start(bf16[96,2048]{1,0:T(8,128)(2,1)} %collective-permute-done.4), channel_id=1, source_target_pairs={{0,16},{8,24},{16,0},{24,8},{1,17},{9,25},{17,1},{25,9},{2,18},{10... | collective-permute-start | bytes 1179656 | tf_op jit(solution)/shard_map/ppermute | solution.py:17
  69.7 24.0 %collective-permute-start.27 = (bf16[4,96,2048]{2,1,0:T(8,128)(2,1)S(1)}, bf16[4,96,2048]{2,1,0:T(8,128)(2,1)S(1)}, u32[]{:S(2)}, u32[]{:S(2)}) collective-permute-start(bf16[4,96,2048]{2,1,0:T(8,128)(2,1)S(1)} %pad_maximum_fusion.refs_1_), channel_id=1, source_target_pairs={{0,1},{1,0},{2,3},{3,2},{4,5},{5,4},{6,7},{7,6},{8,9},{9,8},{10,11... | collective-permute-start | bytes 4718600 | tf_op jit(solution)/shard_map/ppermute | solution.py:17
  69.8 12.3 %collective-permute-start.22 = (bf16[96,2048]{1,0:T(8,128)(2,1)}, bf16[96,2048]{1,0:T(8,128)(2,1)S(1)}, u32[]{:S(2)}, u32[]{:S(2)}) collective-permute-start(bf16[96,2048]{1,0:T(8,128)(2,1)} %collective-permute-done.16), channel_id=1, source_target_pairs={{0,8},{8,0},{16,24},{24,16},{1,9},{9,1},{17,25},{25,17},{2,10},{10... | collective-permute-start | bytes 1179656 | tf_op jit(solution)/shard_map/ppermute | solution.py:17
  71.3 18.9 %collective-permute-start.24 = (bf16[96,2048]{1,0:T(8,128)(2,1)}, bf16[96,2048]{1,0:T(8,128)(2,1)S(1)}, u32[]{:S(2)}, u32[]{:S(2)}) collective-permute-start(bf16[96,2048]{1,0:T(8,128)(2,1)} %collective-permute-done.18), channel_id=1, source_target_pairs={{0,8},{8,0},{16,24},{24,16},{1,9},{9,1},{17,25},{25,17},{2,10},{10... | collective-permute-start | bytes 1179656 | tf_op jit(solution)/shard_map/ppermute | solution.py:17
  75.2 15.4 %collective-permute-start.25 = (f32[3,2048]{1,0:T(4,128)S(1)}, f32[3,2048]{1,0:T(4,128)S(1)}, u32[]{:S(2)}, u32[]{:S(2)}) collective-permute-start(f32[3,2048]{1,0:T(4,128)S(1)} %copy-done.2), channel_id=1, source_target_pairs={{0,24},{8,16},{16,8},{24,0},{1,25},{9,17},{17,9},{25,1},{2,26},{10... | collective-permute-start | bytes 73736 | tf_op jit(solution)/shard_map/ppermute | solution.py:17
  82.0 24.1 %collective-permute-start.14 = (bf16[4,96,2048]{2,1,0:T(8,128)(2,1)S(1)}, bf16[4,96,2048]{2,1,0:T(8,128)(2,1)S(1)}, u32[]{:S(2)}, u32[]{:S(2)}) collective-permute-start(bf16[4,96,2048]{2,1,0:T(8,128)(2,1)S(1)} %pad_maximum_fusion.1.refs_1_), channel_id=1, source_target_pairs={{0,1},{1,0},{2,3},{3,2},{4,5},{5,4},{6,7},{7,6},{8,9},{9,8},{10,11... | collective-permute-start | bytes 4718600 | tf_op jit(solution)/shard_map/ppermute | solution.py:17
  90.3 15.0 %collective-permute-start.20 = (bf16[4,96,2048]{2,1,0:T(8,128)(2,1)S(1)}, bf16[4,96,2048]{2,1,0:T(8,128)(2,1)S(1)}, u32[]{:S(2)}, u32[]{:S(2)}) collective-permute-start(bf16[4,96,2048]{2,1,0:T(8,128)(2,1)S(1)} %pad_maximum_fusion.2.refs_3_.refs_1_), channel_id=1, source_target_pairs={{0,1},{1,0},{2,3},{3,2},{4,5},{5,4},{6,7},{7,6},{8,9},{9,8},{10,11... | collective-permute-start | bytes 4718600 | tf_op jit(solution)/shard_map/ppermute | solution.py:17
  91.2 14.9 %collective-permute-start.26 = (bf16[4,96,2048]{2,1,0:T(8,128)(2,1)S(1)}, bf16[4,96,2048]{2,1,0:T(8,128)(2,1)S(1)}, u32[]{:S(2)}, u32[]{:S(2)}) collective-permute-start(bf16[4,96,2048]{2,1,0:T(8,128)(2,1)S(1)} %pad_maximum_fusion.3.refs_5_.refs_1_), channel_id=1, source_target_pairs={{0,1},{1,0},{2,3},{3,2},{4,5},{5,4},{6,7},{7,6},{8,9},{9,8},{10,11... | collective-permute-start | bytes 4718600 | tf_op jit(solution)/shard_map/ppermute | solution.py:17
  91.7 67.3 %collective-permute-start.37 = (f32[2,32,2048]{2,1,0:T(8,128)S(1)}, f32[2,32,2048]{2,1,0:T(8,128)S(1)}, u32[]{:S(2)}, u32[]{:S(2)}) collective-permute-start(f32[2,32,2048]{2,1,0:T(8,128)S(1)} %get-tuple-element.55), channel_id=1, source_target_pairs={{0,4},{1,5},{2,6},{3,7},{4,0},{5,1},{6,2},{7,3},{8,12},{9,13},{10,... | collective-permute-start | bytes 1572872 | tf_op jit(solution)/shard_map/ppermute | solution.py:17
  93.7 65.3 %collective-permute-start.36 = (f32[2,32,2048]{2,1,0:T(8,128)S(1)}, f32[2,32,2048]{2,1,0:T(8,128)S(1)}, u32[]{:S(2)}, u32[]{:S(2)}) collective-permute-start(f32[2,32,2048]{2,1,0:T(8,128)S(1)} %get-tuple-element.54), channel_id=1, source_target_pairs={{0,2},{1,3},{2,0},{3,1},{4,6},{5,7},{6,4},{7,5},{8,10},{9,11},{10,... | collective-permute-start | bytes 1572872 | tf_op jit(solution)/shard_map/ppermute | solution.py:17
  105.2 53.8 %collective-permute-start.38 = (f32[2,32,2048]{2,1,0:T(8,128)S(1)}, f32[2,32,2048]{2,1,0:T(8,128)S(1)}, u32[]{:S(2)}, u32[]{:S(2)}) collective-permute-start(f32[2,32,2048]{2,1,0:T(8,128)S(1)} %pad_maximum_fusion.12), channel_id=1, source_target_pairs={{0,6},{1,7},{2,4},{3,5},{4,2},{5,3},{6,0},{7,1},{8,14},{9,15},{10,... | collective-permute-start | bytes 1572872 | tf_op jit(solution)/shard_map/ppermute | solution.py:17
  140.1 4.6 %collective-permute-start.30 = (f32[2,8,128]{2,1,0:T(8,128)S(1)}, f32[2,8,128]{2,1,0:T(8,128)S(1)}, u32[]{:S(2)}, u32[]{:S(2)}) collective-permute-start(f32[2,8,128]{2,1,0:T(8,128)S(1)} %get-tuple-element.53.refs_0_), channel_id=1, source_target_pairs={{0,24},{8,16},{16,8},{24,0},{1,25},{9,17},{17,9},{25,1},{2,26},{10... | collective-permute-start | bytes 24584 | tf_op jit(solution)/shard_map/ppermute | solution.py:17
  142.5 3.8 %collective-permute-start.29 = (f32[2,8,128]{2,1,0:T(8,128)S(1)}, f32[2,8,128]{2,1,0:T(8,128)S(1)}, u32[]{:S(2)}, u32[]{:S(2)}) collective-permute-start(f32[2,8,128]{2,1,0:T(8,128)S(1)} %get-tuple-element.53.refs_0_), channel_id=1, source_target_pairs={{0,16},{8,24},{16,0},{24,8},{1,17},{9,25},{17,1},{25,9},{2,18},{10... | collective-permute-start | bytes 24584 | tf_op jit(solution)/shard_map/ppermute | solution.py:17
  144.8 3.7 %collective-permute-start.28 = (f32[2,8,128]{2,1,0:T(8,128)S(1)}, f32[2,8,128]{2,1,0:T(8,128)S(1)}, u32[]{:S(2)}, u32[]{:S(2)}) collective-permute-start(f32[2,8,128]{2,1,0:T(8,128)S(1)} %get-tuple-element.53.refs_0_), channel_id=1, source_target_pairs={{0,8},{8,0},{16,24},{24,16},{1,9},{9,1},{17,25},{25,17},{2,10},{10... | collective-permute-start | bytes 24584 | tf_op jit(solution)/shard_map/ppermute | solution.py:17
  148.5 5.6 %collective-permute-start.33 = (f32[2,8,128]{2,1,0:T(8,128)S(1)}, f32[2,8,128]{2,1,0:T(8,128)S(1)}, u32[]{:S(2)}, u32[]{:S(2)}) collective-permute-start(f32[2,8,128]{2,1,0:T(8,128)S(1)} %merge.3.refs_0_), channel_id=1, source_target_pairs={{0,6},{1,7},{2,4},{3,5},{4,2},{5,3},{6,0},{7,1},{8,14},{9,15},{10,... | collective-permute-start | bytes 24584 | tf_op jit(solution)/shard_map/ppermute | solution.py:17
  151.5 4.5 %collective-permute-start.32 = (f32[2,8,128]{2,1,0:T(8,128)S(1)}, f32[2,8,128]{2,1,0:T(8,128)S(1)}, u32[]{:S(2)}, u32[]{:S(2)}) collective-permute-start(f32[2,8,128]{2,1,0:T(8,128)S(1)} %merge.3.refs_0_), channel_id=1, source_target_pairs={{0,4},{1,5},{2,6},{3,7},{4,0},{5,1},{6,2},{7,3},{8,12},{9,13},{10,... | collective-permute-start | bytes 24584 | tf_op jit(solution)/shard_map/ppermute | solution.py:17
  154.0 3.7 %collective-permute-start.31 = (f32[2,8,128]{2,1,0:T(8,128)S(1)}, f32[2,8,128]{2,1,0:T(8,128)S(1)}, u32[]{:S(2)}, u32[]{:S(2)}) collective-permute-start(f32[2,8,128]{2,1,0:T(8,128)S(1)} %merge.3.refs_0_), channel_id=1, source_target_pairs={{0,2},{1,3},{2,0},{3,1},{4,6},{5,7},{6,4},{7,5},{8,10},{9,11},{10,... | collective-permute-start | bytes 24584 | tf_op jit(solution)/shard_map/ppermute | solution.py:17
  157.7 1.2 collective-permute-start.34
  172.7 10.1 %collective-permute-start.39 = (bf16[1,4,96,2048]{3,2,1,0:T(8,128)(2,1)S(1)}, bf16[1,4,96,2048]{3,2,1,0:T(8,128)(2,1)S(1)}, u32[]{:S(2)}, u32[]{:S(2)}) collective-permute-start(bf16[1,4,96,2048]{3,2,1,0:T(8,128)(2,1)S(1)} %get-tuple-element.60), channel_id=1, source_target_pairs={{0,1},{1,0},{2,3},{3,2},{4,5},{5,4},{6,7},{7,6},{8,9},{9,8},{10,11... | collective-permute-start | bytes 4718600 | tf_op jit(solution)/shard_map/ppermute | solution.py:17
  173.1 9.8 %collective-permute-start.54 = (f32[1,8]{1,0:T(1,128)S(1)}, f32[1,8]{1,0:T(1,128)S(1)}, u32[]{:S(2)}, u32[]{:S(2)}) collective-permute-start(f32[1,8]{1,0:T(1,128)S(1)} %bitcast.185), channel_id=1, source_target_pairs={{0,1},{1,0},{2,3},{3,2},{4,5},{5,4},{6,7},{7,6},{8,9},{9,8},{10,11... | collective-permute-start | bytes 104 | tf_op jit(solution)/shard_map/ppermute | solution.py:17
  182.6 22.9 %collective-permute-start.43 = (bf16[1,4,96,2048]{3,2,1,0:T(8,128)(2,1)S(1)}, bf16[1,4,96,2048]{3,2,1,0:T(8,128)(2,1)S(1)}, u32[]{:S(2)}, u32[]{:S(2)}) collective-permute-start(bf16[1,4,96,2048]{3,2,1,0:T(8,128)(2,1)S(1)} %get-tuple-element.65), channel_id=1, source_target_pairs={{0,1},{1,0},{2,3},{3,2},{4,5},{5,4},{6,7},{7,6},{8,9},{9,8},{10,11... | collective-permute-start | bytes 4718600 | tf_op jit(solution)/shard_map/ppermute | solution.py:17
  183.5 23.0 %collective-permute-start.44 = (bf16[2,96,2048]{2,1,0:T(8,128)(2,1)S(1)}, bf16[2,96,2048]{2,1,0:T(8,128)(2,1)S(1)}, u32[]{:S(2)}, u32[]{:S(2)}) collective-permute-start(bf16[2,96,2048]{2,1,0:T(8,128)(2,1)S(1)} %pad_maximum_fusion.5.refs_4_), channel_id=1, source_target_pairs={{0,8},{8,0},{16,24},{24,16},{1,9},{9,1},{17,25},{25,17},{2,10},{10... | collective-permute-start | bytes 2359304 | tf_op jit(solution)/shard_map/ppermute | solution.py:17
  185.2 23.2 %collective-permute-start.47 = (bf16[2,96,2048]{2,1,0:T(8,128)(2,1)S(1)}, bf16[2,96,2048]{2,1,0:T(8,128)(2,1)S(1)}, u32[]{:S(2)}, u32[]{:S(2)}) collective-permute-start(bf16[2,96,2048]{2,1,0:T(8,128)(2,1)S(1)} %pad_maximum_fusion.6.refs_5_), channel_id=1, source_target_pairs={{0,16},{8,24},{16,0},{24,8},{1,17},{9,25},{17,1},{25,9},{2,18},{10... | collective-permute-start | bytes 2359304 | tf_op jit(solution)/shard_map/ppermute | solution.py:17
  195.7 13.6 %collective-permute-start.41 = (bf16[1,4,96,2048]{3,2,1,0:T(8,128)(2,1)S(1)}, bf16[1,4,96,2048]{3,2,1,0:T(8,128)(2,1)S(1)}, u32[]{:S(2)}, u32[]{:S(2)}) collective-permute-start(bf16[1,4,96,2048]{3,2,1,0:T(8,128)(2,1)S(1)} %get-tuple-element.64), channel_id=1, source_target_pairs={{0,1},{1,0},{2,3},{3,2},{4,5},{5,4},{6,7},{7,6},{8,9},{9,8},{10,11... | collective-permute-start | bytes 4718600 | tf_op jit(solution)/shard_map/ppermute | solution.py:17
  204.9 5.6 %collective-permute-start.40 = (bf16[1,4,96,2048]{3,2,1,0:T(8,128)(2,1)S(1)}, bf16[1,4,96,2048]{3,2,1,0:T(8,128)(2,1)S(1)}, u32[]{:S(2)}, u32[]{:S(2)}) collective-permute-start(bf16[1,4,96,2048]{3,2,1,0:T(8,128)(2,1)S(1)} %get-tuple-element.63), channel_id=1, source_target_pairs={{0,1},{1,0},{2,3},{3,2},{4,5},{5,4},{6,7},{7,6},{8,9},{9,8},{10,11... | collective-permute-start | bytes 4718600 | tf_op jit(solution)/shard_map/ppermute | solution.py:17
  205.8 48.4 %collective-permute-start.49 = (bf16[1,96,2048]{2,1,0:T(8,128)(2,1)S(1)}, bf16[1,96,2048]{2,1,0:T(8,128)(2,1)S(1)}, u32[]{:S(2)}, u32[]{:S(2)}) collective-permute-start(bf16[1,96,2048]{2,1,0:T(8,128)(2,1)S(1)} %get-tuple-element.84.refs_8_), channel_id=1, source_target_pairs={{0,16},{8,24},{16,0},{24,8},{1,17},{9,25},{17,1},{25,9},{2,18},{10... | collective-permute-start | bytes 1179656 | tf_op jit(solution)/shard_map/ppermute | solution.py:17
  207.0 35.7 %collective-permute-start.45 = (bf16[1,96,2048]{2,1,0:T(8,128)(2,1)S(1)}, bf16[1,96,2048]{2,1,0:T(8,128)(2,1)S(1)}, u32[]{:S(2)}, u32[]{:S(2)}) collective-permute-start(bf16[1,96,2048]{2,1,0:T(8,128)(2,1)S(1)} %get-tuple-element.80.refs_6_), channel_id=1, source_target_pairs={{0,16},{8,24},{16,0},{24,8},{1,17},{9,25},{17,1},{25,9},{2,18},{10... | collective-permute-start | bytes 1179656 | tf_op jit(solution)/shard_map/ppermute | solution.py:17
  208.4 33.7 %collective-permute-start.52 = (bf16[2,96,2048]{2,1,0:T(8,128)(2,1)S(1)}, bf16[2,96,2048]{2,1,0:T(8,128)(2,1)S(1)}, u32[]{:S(2)}, u32[]{:S(2)}) collective-permute-start(bf16[2,96,2048]{2,1,0:T(8,128)(2,1)S(1)} %pad_maximum_fusion.8.refs_10_), channel_id=1, source_target_pairs={{0,16},{8,24},{16,0},{24,8},{1,17},{9,25},{17,1},{25,9},{2,18},{10... | collective-permute-start | bytes 2359304 | tf_op jit(solution)/shard_map/ppermute | solution.py:17
  209.6 44.5 %collective-permute-start.48 = (bf16[1,96,2048]{2,1,0:T(8,128)(2,1)S(1)}, bf16[1,96,2048]{2,1,0:T(8,128)(2,1)S(1)}, u32[]{:S(2)}, u32[]{:S(2)}) collective-permute-start(bf16[1,96,2048]{2,1,0:T(8,128)(2,1)S(1)} %get-tuple-element.82.refs_7_), channel_id=1, source_target_pairs={{0,8},{8,0},{16,24},{24,16},{1,9},{9,1},{17,25},{25,17},{2,10},{10... | collective-permute-start | bytes 1179656 | tf_op jit(solution)/shard_map/ppermute | solution.py:17
  210.5 32.3 %collective-permute-start.42 = (bf16[1,96,2048]{2,1,0:T(8,128)(2,1)S(1)}, bf16[1,96,2048]{2,1,0:T(8,128)(2,1)S(1)}, u32[]{:S(2)}, u32[]{:S(2)}) collective-permute-start(bf16[1,96,2048]{2,1,0:T(8,128)(2,1)S(1)} %get-tuple-element.86.refs_5_), channel_id=1, source_target_pairs={{0,8},{8,0},{16,24},{24,16},{1,9},{9,1},{17,25},{25,17},{2,10},{10... | collective-permute-start | bytes 1179656 | tf_op jit(solution)/shard_map/ppermute | solution.py:17
  242.2 18.6 %collective-permute-start.51 = (bf16[2,96,2048]{2,1,0:T(8,128)(2,1)S(1)}, bf16[2,96,2048]{2,1,0:T(8,128)(2,1)S(1)}, u32[]{:S(2)}, u32[]{:S(2)}) collective-permute-start(bf16[2,96,2048]{2,1,0:T(8,128)(2,1)S(1)} %pad_maximum_fusion.7.refs_9_), channel_id=1, source_target_pairs={{0,8},{8,0},{16,24},{24,16},{1,9},{9,1},{17,25},{25,17},{2,10},{10... | collective-permute-start | bytes 2359304 | tf_op jit(solution)/shard_map/ppermute | solution.py:17
  243.0 11.2 %collective-permute-start.46 = (bf16[96,2048]{1,0:T(8,128)(2,1)S(1)}, bf16[96,2048]{1,0:T(8,128)(2,1)S(1)}, u32[]{:S(2)}, u32[]{:S(2)}) collective-permute-start(bf16[96,2048]{1,0:T(8,128)(2,1)S(1)} %fusion.24.refs_4_), channel_id=1, source_target_pairs={{0,2},{1,3},{2,0},{3,1},{4,6},{5,7},{6,4},{7,5},{8,10},{9,11},{10,... | collective-permute-start | bytes 1179656 | tf_op jit(solution)/shard_map/ppermute | solution.py:17
  243.1 11.1 %collective-permute-start.55 = (f32[1,8]{1,0:T(1,128)S(1)}, f32[1,8]{1,0:T(1,128)S(1)}, u32[]{:S(2)}, u32[]{:S(2)}) collective-permute-start(f32[1,8]{1,0:T(1,128)S(1)} %add.316), channel_id=1, source_target_pairs={{0,2},{1,3},{2,0},{3,1},{4,6},{5,7},{6,4},{7,5},{8,10},{9,11},{10,... | collective-permute-start | bytes 104 | tf_op jit(solution)/shard_map/ppermute | solution.py:17
  254.5 19.0 %collective-permute-start.50 = (bf16[96,2048]{1,0:T(8,128)(2,1)S(1)}, bf16[96,2048]{1,0:T(8,128)(2,1)S(1)}, u32[]{:S(2)}, u32[]{:S(2)}) collective-permute-start(bf16[96,2048]{1,0:T(8,128)(2,1)S(1)} %add_convert_fusion.3.refs_4_), channel_id=1, source_target_pairs={{0,4},{1,5},{2,6},{3,7},{4,0},{5,1},{6,2},{7,3},{8,12},{9,13},{10,... | collective-permute-start | bytes 1179656 | tf_op jit(solution)/shard_map/ppermute | solution.py:17
  256.2 17.2 %collective-permute-start.56 = (f32[1,8]{1,0:T(1,128)S(1)}, f32[1,8]{1,0:T(1,128)S(1)}, u32[]{:S(2)}, u32[]{:S(2)}) collective-permute-start(f32[1,8]{1,0:T(1,128)S(1)} %add.317), channel_id=1, source_target_pairs={{0,4},{1,5},{2,6},{3,7},{4,0},{5,1},{6,2},{7,3},{8,12},{9,13},{10,... | collective-permute-start | bytes 104 | tf_op jit(solution)/shard_map/ppermute | solution.py:17
  261.0 17.3 %collective-permute-start.53 = (bf16[96,2048]{1,0:T(8,128)(2,1)S(1)}, bf16[96,2048]{1,0:T(8,128)(2,1)S(1)}, u32[]{:S(2)}, u32[]{:S(2)}) collective-permute-start(bf16[96,2048]{1,0:T(8,128)(2,1)S(1)} %add_convert_fusion.refs_4_), channel_id=1, source_target_pairs={{0,2},{1,3},{2,0},{3,1},{4,6},{5,7},{6,4},{7,5},{8,10},{9,11},{10,... | collective-permute-start | bytes 1179656 | tf_op jit(solution)/shard_map/ppermute | solution.py:17
  279.0 13.2 %copy-start.11 = (f32[3,32]{1,0:T(4,128)S(1)}, f32[3,32]{1,0:T(4,128)}, u32[]{:S(2)}) copy-start(f32[3,32]{1,0:T(4,128)} %copy-done.10) | copy-start | bytes 1156
  279.0 13.2 %copy-start.12 = (f32[3,32]{1,0:T(4,128)S(1)}, f32[3,32]{1,0:T(4,128)}, u32[]{:S(2)}) copy-start(f32[3,32]{1,0:T(4,128)} %get-tuple-element.77) | copy-start | bytes 1156
  279.0 12.6 %collective-permute-start.58 = (f32[4,32]{1,0:T(4,128)S(1)}, f32[4,32]{1,0:T(4,128)S(1)}, u32[]{:S(2)}, u32[]{:S(2)}) collective-permute-start(f32[4,32]{1,0:T(4,128)S(1)} %select_maximum_fusion), channel_id=1, source_target_pairs={{0,16},{8,24},{16,0},{24,8},{1,17},{9,25},{17,1},{25,9},{2,18},{10... | collective-permute-start | bytes 1544 | tf_op jit(solution)/shard_map/ppermute | solution.py:17
  279.9 11.7 %collective-permute-start.59 = (f32[4,32]{1,0:T(4,128)S(1)}, f32[4,32]{1,0:T(4,128)S(1)}, u32[]{:S(2)}, u32[]{:S(2)}) collective-permute-start(f32[4,32]{1,0:T(4,128)S(1)} %select_maximum_fusion), channel_id=1, source_target_pairs={{0,24},{8,16},{16,8},{24,0},{1,25},{9,17},{17,9},{25,1},{2,26},{10... | collective-permute-start | bytes 1544 | tf_op jit(solution)/shard_map/ppermute | solution.py:17
  281.1 10.5 %collective-permute-start.57 = (f32[4,32]{1,0:T(4,128)S(1)}, f32[4,32]{1,0:T(4,128)S(1)}, u32[]{:S(2)}, u32[]{:S(2)}) collective-permute-start(f32[4,32]{1,0:T(4,128)S(1)} %select_maximum_fusion), channel_id=1, source_target_pairs={{0,8},{8,0},{16,24},{24,16},{1,9},{9,1},{17,25},{25,17},{2,10},{10... | collective-permute-start | bytes 1544 | tf_op jit(solution)/shard_map/ppermute | solution.py:17
  (9 other events, 21.3 us)
